TPU v7x, 256 devices: a whole 4x4x8 slice. The times are simulated.
256 devices in a mesh: seq: 8 (over z), expert: 8 (over y, core), mp: 4 (over x).
Axes of the slice: x: 4, y: 4, z: 8, core: 2. Of those that a mesh axis runs over, the one named last changes fastest.
Arguments:
- tokens: bfloat16 [2048, 6144], P(('seq', 'expert', 'mp')), may hold values from -6 to 6
- out_grad: bfloat16 [2048, 6144], P(('seq', 'expert', 'mp')), may hold values from -3 to 3
- kept_mask: int32 [2048], P(('seq', 'expert', 'mp')), may hold values 0 or 1
- routes: int32 [2048, 2], P(('seq', 'expert', 'mp')), may hold values from 0 to 7, all different within a row; in each aligned block of 8 rows (0 to 7, 8 to 15, ...) at most 3 rows name the same one
- router: bfloat16 [6144, 8], replicated, may hold values from -0.078125 to 0.078125
- gate_weight: bfloat16 [8, 6144, 8192], P('expert', None, ('seq', 'mp')), may hold values from -0.078125 to 0.078125
- up_weight: bfloat16 [8, 6144, 8192], P('expert', None, ('seq', 'mp')), may hold values from -0.078125 to 0.078125
- down_weight: bfloat16 [8, 8192, 6144], P('expert', ('seq', 'mp')), may hold values from -0.0625 to 0.0625
Outputs:
- d_tokens: bfloat16 [2048, 6144], P(('seq', 'expert', 'mp'))
- gate_grad: float32 [2048, 2], P(('seq', 'expert', 'mp'))
Inputs may be any that keep to these rules, and one draw needn't show every extreme that they name: `routes`: among the 8 rows of one device, at most 3 name any one expert, and in every draw some expert is named by exactly 3 rows of some device.
All inputs are finite; a program needn't handle non-finite values. No bound on the sum of `kept_mask` on one device may be relied on, other than what follows from the above.
Results may differ from a plain program's by a relative error of at most 0.02.
Values may be sent and summed in bfloat16 or wider, within the bound.
A program may use at most 128 MiB of HBM per device.

v0:
```python
import jax
import jax.numpy as jnp
from jax import lax
from jax.sharding import PartitionSpec as P


def on_device(tokens, out_grad, kept_mask, routes, router, gate_weight, up_weight, down_weight):
    row_count = tokens.shape[0]
    width = tokens.shape[1]
    expert_count = lax.axis_size("expert")
    capacity = max(3 * row_count // 8, 2 * row_count // expert_count)
    logits = jnp.dot(tokens, router, preferred_element_type=jnp.float32)
    columns = lax.broadcasted_iota(jnp.int32, (row_count, expert_count), 1)
    first_hot = (routes[:, 0:1] == columns).astype(jnp.float32)
    second_hot = (routes[:, 1:2] == columns).astype(jnp.float32)
    first_logit = jnp.sum(logits * first_hot, axis=1)
    second_logit = jnp.sum(logits * second_hot, axis=1)
    gate_first = jax.nn.sigmoid(first_logit - second_logit)
    gate_second = jax.nn.sigmoid(second_logit - first_logit)
    keep_rows = kept_mask.astype(jnp.float32)
    chosen = ((first_hot + second_hot) * keep_rows[:, None]).astype(jnp.int32)
    position = jnp.cumsum(chosen, axis=0) - 1
    slot_iota = lax.broadcasted_iota(jnp.int32, (row_count, expert_count, capacity), 2)
    select_mask = (chosen[:, :, None] == 1) & (position[:, :, None] == slot_iota)
    select_bf = select_mask.astype(jnp.bfloat16)
    select_full = select_mask.astype(jnp.float32)
    token_send = jnp.einsum(
        "tec,td->ecd", select_bf, tokens, preferred_element_type=jnp.float32
    ).astype(jnp.bfloat16)
    grad_send = jnp.einsum(
        "tec,td->ecd", select_bf, out_grad, preferred_element_type=jnp.float32
    ).astype(jnp.bfloat16)
    gate_table = first_hot * gate_first[:, None] + second_hot * gate_second[:, None]
    gate_send = jnp.einsum(
        "tec,te->ec", select_full, gate_table, precision=lax.Precision.HIGHEST
    ).astype(jnp.bfloat16)
    token_recv, grad_recv, gate_recv = (
        lax.all_to_all(token_send, "expert", split_axis=0, concat_axis=0, tiled=True),
        lax.all_to_all(grad_send, "expert", split_axis=0, concat_axis=0, tiled=True),
        lax.all_to_all(gate_send, "expert", split_axis=0, concat_axis=0, tiled=True),
    )
    token_all, grad_all, gate_all = (
        lax.all_gather(token_recv, ("seq", "mp"), axis=0, tiled=True),
        lax.all_gather(grad_recv, ("seq", "mp"), axis=0, tiled=True),
        lax.all_gather(gate_recv, ("seq", "mp"), axis=0, tiled=True),
    )
    token_all = token_all.reshape(-1, width)
    grad_all = grad_all.reshape(-1, width)
    gate_all = gate_all.reshape(-1)
    gate_local = gate_weight[0]
    up_local = up_weight[0]
    down_local = down_weight[0]
    pre_gate = jnp.dot(token_all, gate_local, preferred_element_type=jnp.float32)
    pre_up = jnp.dot(token_all, up_local, preferred_element_type=jnp.float32)
    sigma = jax.nn.sigmoid(pre_gate)
    act = pre_gate * sigma
    hidden = act * pre_up
    grad_hidden = jnp.dot(grad_all, down_local.T, preferred_element_type=jnp.float32)
    gate_dot = jnp.sum(grad_hidden * hidden, axis=1)
    scaled = gate_all.astype(jnp.float32)[:, None] * grad_hidden
    grad_gate = (scaled * pre_up * sigma * (1.0 + pre_gate * (1.0 - sigma))).astype(jnp.bfloat16)
    grad_up = (scaled * act).astype(jnp.bfloat16)
    expert_grad = jnp.dot(grad_gate, gate_local.T, preferred_element_type=jnp.float32)
    expert_grad = expert_grad + jnp.dot(grad_up, up_local.T, preferred_element_type=jnp.float32)
    grad_own = lax.psum_scatter(
        expert_grad.astype(jnp.bfloat16), ("seq", "mp"), scatter_dimension=0, tiled=True
    ).astype(jnp.float32)
    dot_own = lax.psum_scatter(gate_dot, ("seq", "mp"), scatter_dimension=0, tiled=True)
    grad_back, dot_back = (
        lax.all_to_all(
            grad_own.reshape(expert_count, capacity, width).astype(jnp.bfloat16),
            "expert",
            split_axis=0,
            concat_axis=0,
            tiled=True,
        ).astype(jnp.float32),
        lax.all_to_all(
            dot_own.reshape(expert_count, capacity).astype(jnp.bfloat16),
            "expert",
            split_axis=0,
            concat_axis=0,
            tiled=True,
        ).astype(jnp.float32),
    )
    expert_sum = jnp.einsum("tec,ecd->td", select_full, grad_back, precision=lax.Precision.HIGHEST)
    dot_table = jnp.einsum("tec,ec->te", select_full, dot_back, precision=lax.Precision.HIGHEST)
    dot_first = jnp.sum(dot_table * first_hot, axis=1)
    dot_second = jnp.sum(dot_table * second_hot, axis=1)
    product = gate_first * gate_second * keep_rows
    grad_first = product * (dot_first - dot_second)
    grad_second = product * (dot_second - dot_first)
    logit_grad = first_hot * grad_first[:, None] + second_hot * grad_second[:, None]
    router_term = jnp.dot(logit_grad, router.astype(jnp.float32).T, precision=lax.Precision.HIGHEST)
    d_tokens = ((expert_sum + router_term) * keep_rows[:, None]).astype(jnp.bfloat16)
    gate_grad = jnp.stack([grad_first, grad_second], axis=1)
    return (d_tokens, gate_grad)


def solution(mesh):
    return jax.shard_map(
        on_device,
        mesh=mesh,
        in_specs=(
            P(("seq", "expert", "mp"), None),
            P(("seq", "expert", "mp"), None),
            P(("seq", "expert", "mp")),
            P(("seq", "expert", "mp"), None),
            P(),
            P("expert", None, ("seq", "mp")),
            P("expert", None, ("seq", "mp")),
            P("expert", ("seq", "mp"), None),
        ),
        out_specs=(P(("seq", "expert", "mp"), None), P(("seq", "expert", "mp"), None)),
        check_vma=False,
    )
```

profile of v0, /device:TPU:1, one launch (start us, length us, event | category | flops | bytes accessed | tf_op | source)
XLA Modules:
  0.0 688.7 jit_solution(3209703216275535613)
XLA Ops:
  7.2 0.8 slice_bitcast_fusion.1
  8.1 0.7 convert_element_type.92
  9.7 1.2 convolution_convert_fusion
  11.1 13.9 %all_to_all.36 = bf16[8,3,6144]{2,1,0:T(4,128)(2,1)S(1)} all-to-all(bf16[8,3,6144]{2,1,0:T(4,128)(2,1)S(1)} %copy.43), channel_id=1, replica_groups=mesh['seq'=8,'expert'=8,'mp'=4] {'expert'}, dimensions={0} | all-to-all | bytes 589824 | tf_op jit(solution)/shard_map/all_to_all | solution.py:38
  24.9 0.9 copy.44
  26.0 1.2 convolution_convert_fusion.1
  27.4 11.3 %all_to_all.37 = bf16[8,3,6144]{2,1,0:T(4,128)(2,1)S(1)} all-to-all(bf16[8,3,6144]{2,1,0:T(4,128)(2,1)S(1)} %copy.39), channel_id=1, replica_groups=mesh['seq'=8,'expert'=8,'mp'=4] {'expert'}, dimensions={0} | all-to-all | bytes 589824 | tf_op jit(solution)/shard_map/all_to_all | solution.py:39
  38.7 0.9 copy.40
  39.7 1.3 dynamic-slice
  41.7 88.6 %all-gather.6.cloned.1.call-done = bf16[256,3,6144]{2,0,1:T(8,128)(2,1)} async-done(((bf16[8,3,6144]{2,0,1:T(8,128)(2,1)}), bf16[256,3,6144]{2,0,1:T(8,128)(2,1)}) %all-gather.6.cloned.1.call-update) | async-done | bytes 9437200 | tf_op jit(solution)/shard_map/all_gather | solution.py:43
  130.3 14.7 %copy.45 = bf16[256,3,6144]{2,1,0:T(4,128)(2,1)} copy(bf16[256,3,6144]{2,0,1:T(8,128)(2,1)} %all-gather.6.cloned.1.call-done) | data formatting | bytes 18874368 | tf_op jit(solution)/shard_map/all_gather | solution.py:43
  145.0 23.6 %reshape.179 = bf16[768,6144]{1,0:T(8,128)(2,1)} reshape(bf16[256,3,6144]{2,1,0:T(4,128)(2,1)} %copy.45) | data formatting | bytes 18874368 | tf_op jit(solution)/shard_map/reshape | solution.py:47
  168.5 7.4 %fusion.4 = f32[768,256]{0,1:T(8,128)} fusion(bf16[768,6144]{1,0:T(8,128)(2,1)} %reshape.179, bf16[1,6144,256]{2,1,0:T(8,128)(2,1)S(1)} %copy-done), kind=kOutput, calls=%fused_computation.9 | convolution fusion | flops 2415919104 | bytes 13369344 | tf_op jit(solution)/shard_map/dot_general | solution.py:53
  175.9 3.8 fusion.7
  179.7 53.8 %all-gather.4.cloned.1.call-done = bf16[256,3,6144]{2,0,1:T(8,128)(2,1)} async-done(((bf16[8,3,6144]{2,0,1:T(8,128)(2,1)}), bf16[256,3,6144]{2,0,1:T(8,128)(2,1)}) %all-gather.4.cloned.1.call-update) | async-done | bytes 9437200 | tf_op jit(solution)/shard_map/all_gather | solution.py:44
  233.5 14.7 %copy.41 = bf16[256,3,6144]{2,1,0:T(4,128)(2,1)} copy(bf16[256,3,6144]{2,0,1:T(8,128)(2,1)} %all-gather.4.cloned.1.call-done) | data formatting | bytes 18874368 | tf_op jit(solution)/shard_map/all_gather | solution.py:44
  248.2 23.5 %reshape.178 = bf16[768,6144]{1,0:T(8,128)(2,1)} reshape(bf16[256,3,6144]{2,1,0:T(4,128)(2,1)} %copy.41) | data formatting | bytes 18874368 | tf_op jit(solution)/shard_map/reshape | solution.py:48
  271.7 8.6 %multiply_reduce_fusion = (f32[768]{0:T(1024)S(1)}, f32[768,256]{0,1:T(8,128)}) fusion(f32[768,256]{0,1:T(8,128)} %fusion.7, f32[768,256]{0,1:T(8,128)} %fusion.4, bf16[768,6144]{1,0:T(8,128)(2,1)} %reshape.178, bf16[1,256,6144]{2,1,0:T(8,128)(2,1)} %param.15), kind=kOutput, calls=%fused_computation.16 | convolution fusion | flops 2417294592 | bytes 14945280 | tf_op jit(solution)/shard_map/dot_general | solution.py:58
  280.3 57.6 %all-reduce = bf16[768]{0:T(1024)(128)(2,1)S(1)} all-reduce(f32[768]{0:T(1024)S(1)} %get-tuple-element.13), channel_id=4, replica_groups=mesh['seq'=8,'expert'=8,'mp'=4] {'seq','mp'}, use_global_device_ids=true, to_apply=%region_5.6.clone | all-reduce | flops 768 | bytes 4608
  338.0 23.4 %all_to_all.38 = bf16[8,1,3]{2,1,0:T(2,128)(2,1)S(1)} all-to-all(bf16[8,1,3]{2,1,0:T(2,128)(2,1)S(1)} %convert_element_type.108), channel_id=1, replica_groups=mesh['seq'=8,'expert'=8,'mp'=4] {'expert'}, dimensions={0} | all-to-all | bytes 96 | tf_op jit(solution)/shard_map/all_to_all | solution.py:77
  361.8 0.5 subtract_multiply_fusion.1
  362.6 7.6 %all_to_all.39 = bf16[8,1,3]{2,1,0:T(2,128)(2,1)S(1)} all-to-all(bf16[8,1,3]{2,1,0:T(2,128)(2,1)S(1)} %copy.37), channel_id=1, replica_groups=mesh['seq'=8,'expert'=8,'mp'=4] {'expert'}, dimensions={0} | all-to-all | bytes 96 | tf_op jit(solution)/shard_map/all_to_all | solution.py:40
  370.2 30.7 %all-gather = bf16[256,1,3]{2,1,0:T(2,128)(2,1)S(1)} all-gather(bf16[8,1,3]{2,1,0:T(2,128)(2,1)S(1)} %all_to_all.39), channel_id=2, replica_groups=mesh['seq'=8,'expert'=8,'mp'=4] {'seq','mp'}, dimensions={0}, use_global_device_ids=true | all-gather | bytes 1584 | tf_op jit(solution)/shard_map/all_gather | solution.py:45
  401.5 9.7 %fusion.2 = f32[768,6144]{1,0:T(8,128)} fusion(bf16[1,6144,256]{2,1,0:T(8,128)(2,1)S(1)} %copy-done, f32[768,256]{0,1:T(8,128)} %fusion.4, f32[768,256]{0,1:T(8,128)} %fusion.7, f32[768,256]{0,1:T(8,128)} %get-tuple-element.14, f32[768]{0:T(1024)S(1)} %reshape.180), kind=kOutput, calls=%fused_computation.7 | convolution fusion | flops 2418081792 | bytes 24382464 | tf_op jit(solution)/shard_map/dot_general | solution.py:63
  411.2 14.2 %add_convert_fusion = bf16[768,6144]{1,0:T(8,128)(2,1)} fusion(f32[768,6144]{1,0:T(8,128)} %fusion.2, bf16[1,6144,256]{2,1,0:T(8,128)(2,1)} %param.14, f32[768,256]{0,1:T(8,128)} %get-tuple-element.14, f32[768]{0:T(1024)S(1)} %reshape.180, f32[768,256]{0,1:T(8,128)} %fusion.4), kind=kOutput, calls=%fused_computation | convolution fusion | flops 2426732544 | bytes 33033216 | tf_op jit(solution)/shard_map/dot_general | solution.py:64
  425.5 235.6 %reduce-scatter.2.cloned.1.call-done = bf16[24,6144]{1,0:T(8,128)(2,1)} async-done(((bf16[768,6144]{1,0:T(8,128)(2,1)}), bf16[24,6144]{1,0:T(8,128)(2,1)}) %reduce-scatter.2.cloned.1.call-update) | async-done | bytes 294928 | tf_op jit(solution)/shard_map/reduce_scatter | solution.py:65
  661.1 1.9 convert_element_type.102
  662.9 9.0 %all-to-all-start.3 = ((bf16[8,3,6144]{2,1,0:T(4,128)(2,1)}), bf16[8,3,6144]{2,1,0:T(4,128)(2,1)S(1)}, u32[]{:S(2)}, u32[]{:S(2)}) async-start(bf16[8,3,6144]{2,1,0:T(4,128)(2,1)} %convert_element_type.102), calls=%async_computation.4 | async-start | bytes 786432 | tf_op jit(solution)/shard_map/all_to_all | solution.py:70
  671.9 0.7 subtract_multiply_fusion
  673.2 1.2 pad_maximum_fusion
  674.3 5.7 all-to-all-done.3
  680.3 1.8 fusion.1
  (52 shorter events, 3.7 us)
Async XLA Ops:
  7.2 161.4 %copy-start = (bf16[1,6144,256]{2,1,0:T(8,128)(2,1)S(1)}, bf16[1,6144,256]{2,1,0:T(8,128)(2,1)}, u32[]{:S(2)}) copy-start(bf16[1,6144,256]{2,1,0:T(8,128)(2,1)} %param.13) | copy-start | bytes 9437188
  7.2 123.1 %all-gather.6.cloned.1.call-start = ((), (), s32[]{:S(2)}) async-start(), calls=%async_computation.7 | async-start | bytes 9732096 | tf_op jit(solution)/shard_map/all_gather | solution.py:43
  8.8 0.5 copy-start.5
  25.9 207.6 %all-gather.4.cloned.1.call-start = ((), (), s32[]{:S(2)}) async-start(), calls=%async_computation.6 | async-start | bytes 9732096 | tf_op jit(solution)/shard_map/all_gather | solution.py:44
  39.7 621.4 %reduce-scatter.2.cloned.1.call-start = ((), (), s32[]{:S(2)}) async-start(), calls=%async_computation.8 | async-start | bytes 9732096 | tf_op jit(solution)/shard_map/reduce_scatter | solution.py:65
  168.5 7.4 %copy-start.1 = (bf16[768,6144]{1,0:T(8,128)(2,1)S(1)}, bf16[768,6144]{1,0:T(8,128)(2,1)}, u32[]{:S(2)}) copy-start(bf16[768,6144]{1,0:T(8,128)(2,1)} %reshape.179) | copy-start | bytes 28311556
  168.5 7.4 %copy-start.2 = (bf16[1,6144,256]{2,1,0:T(8,128)(2,1)S(1)}, bf16[1,6144,256]{2,1,0:T(8,128)(2,1)}, u32[]{:S(2)}) copy-start(bf16[1,6144,256]{2,1,0:T(8,128)(2,1)} %param.14) | copy-start | bytes 9437188
  271.7 89.9 %copy-start.3 = (bf16[8,6144]{1,0:T(8,128)(2,1)S(1)}, bf16[8,6144]{1,0:T(8,128)(2,1)}, u32[]{:S(2)}) copy-start(bf16[8,6144]{1,0:T(8,128)(2,1)} %param.8) | copy-start | bytes 294916
  271.7 89.9 %copy-start.4 = (bf16[6144,8]{0,1:T(8,128)(2,1)S(1)}, bf16[6144,8]{0,1:T(8,128)(2,1)}, u32[]{:S(2)}) copy-start(bf16[6144,8]{0,1:T(8,128)(2,1)} %param.12) | copy-start | bytes 294916
  271.7 90.1 %copy-start.11 = (s32[8]{0:T(128)S(1)}, s32[8]{0:T(128)}, u32[]{:S(2)}) copy-start(s32[8]{0:T(128)} %param.10) | copy-start | bytes 100
  361.8 49.4 %copy-start.7 = (f32[8]{0:T(128)}, f32[8]{0:T(128)S(1)}, u32[]{:S(2)}) copy-start(f32[8]{0:T(128)S(1)} %get-tuple-element.6) | copy-start | bytes 100
  361.8 49.3 %copy-start.8 = (f32[8]{0:T(128)}, f32[8]{0:T(128)S(1)}, u32[]{:S(2)}) copy-start(f32[8]{0:T(128)S(1)} %get-tuple-element.7) | copy-start | bytes 100
  362.4 48.8 %copy-start.9 = (f32[8]{0:T(128)}, f32[8]{0:T(128)S(1)}, u32[]{:S(2)}) copy-start(f32[8]{0:T(128)S(1)} %get-tuple-element.9) | copy-start | bytes 100
  362.4 48.8 %copy-start.10 = (f32[8]{0:T(128)}, f32[8]{0:T(128)S(1)}, u32[]{:S(2)}) copy-start(f32[8]{0:T(128)S(1)} %get-tuple-element.10) | copy-start | bytes 100
  662.9 17.0 %all-to-all-start.3 = ((bf16[8,3,6144]{2,1,0:T(4,128)(2,1)}), bf16[8,3,6144]{2,1,0:T(4,128)(2,1)S(1)}, u32[]{:S(2)}, u32[]{:S(2)}) async-start(bf16[8,3,6144]{2,1,0:T(4,128)(2,1)} %convert_element_type.102), calls=%async_computation.4 | async-start | bytes 786432 | tf_op jit(solution)/shard_map/all_to_all | solution.py:70
  672.6 0.5 copy-start.6
Sparse Core Ops, SparseCore 0:
  26.0 104.1 all-gather.5
  132.9 100.5 all-gather.3
  425.6 235.4 reduce-scatter.1
where the time goes:
time: 690 us; the launch traced here: 689 us
  waiting for transfers between devices  384 us (56%)
  blocking collectives  144 us (21%)
  local copies, waits for them, and re-layouts  84.8 us (12%)
  matrix products  48.3 us (7%)
  between operations  14.5 us (2%)
  starting transfers between devices  9.09 us (1%)
    reduce_scatter x1, waiting for transfers between devices, on_device(): lax.psum_scatter(expert_grad.astype(jnp.bfloat16), ('seq', 'mp'), scatter...  236 us
    all_gather x1, waiting for transfers between devices, on_device(): lax.all_gather(token_recv, ('seq', 'mp'), axis=0, tiled=True)  88.6 us
    unnamed x1, blocking collectives  57.6 us
    all_gather x1, waiting for transfers between devices, on_device(): lax.all_gather(grad_recv, ('seq', 'mp'), axis=0, tiled=True)  53.8 us
    all_gather x1, blocking collectives, on_device(): lax.all_gather(gate_recv, ('seq', 'mp'), axis=0, tiled=True)  30.7 us
    reshape x1, local copies, waits for them, and re-layouts, on_device(): token_all = token_all.reshape(-1, width)  23.6 us
    reshape x1, local copies, waits for them, and re-layouts, on_device(): grad_all = grad_all.reshape(-1, width)  23.5 us
    all_to_all x1, blocking collectives, on_device(): lax.all_to_all(dot_own.reshape(expert_count, capacity).astype(jnp.bfloat1...  23.4 us
  transfers between devices with their start and end apart: 4, of which 4 were waited for; matrix products, arithmetic and copies ran while one was open for 8% of the time, Pallas kernels for 0%

commit v1 on v0

v1 whole, which is shorter than its diff:
```python
import functools

import jax
import jax.numpy as jnp
from jax import lax
from jax.experimental import pallas as pl
from jax.experimental.pallas import tpu as pltpu
from jax.sharding import PartitionSpec as P

MESH = pl.DeviceIdType.MESH
BF = jnp.bfloat16
F32 = jnp.float32
RING = 32
GROUP = 4
SPAN = 8


def div(a, b):
    return a // b if isinstance(a, int) else lax.div(a, jnp.int32(b))


def rem(a, b):
    return a % b if isinstance(a, int) else lax.rem(a, jnp.int32(b))


def place(cycle, z, x):
    if cycle == 0:
        return 4 * z + rem(x + z, 4)
    turn = rem(z + 5 * x, 8)
    return 4 * x + 16 * div(turn, 4) + rem(turn, 4)


def coords(cycle, q):
    a, b = div(q, 4), rem(q, 4)
    if cycle == 0:
        return a, rem(b - a + 8, 4)
    return rem(3 * a + b, 8), rem(a, 4)


def peer(z, x):
    return {"seq": z, "mp": x}


def dispatch_kernel(count, send_ref, recv_ref, send_sem, recv_sem, own_sem):
    z, e, x = lax.axis_index("seq"), lax.axis_index("expert"), lax.axis_index("mp")
    other = x + 1 - 2 * rem(x, 2)
    kind = rem(x + z, 2)
    slot = rem(x, 2) * count + e

    def target(j, mine):
        return {"seq": z, "expert": rem(e + j, count), "mp": x if mine else other}

    barrier = pltpu.get_barrier_semaphore()
    for j in range(count):
        if j:
            pl.semaphore_signal(barrier, inc=1, device_id=target(j, True), device_id_type=MESH)
        pl.semaphore_signal(barrier, inc=1, device_id=target(j, False), device_id_type=MESH)
    pl.semaphore_wait(barrier, 2 * count - 1)

    local = pltpu.make_async_copy(send_ref.at[kind, e], recv_ref.at[slot], own_sem)
    local.start()
    copies = []
    for j in range(count):
        for mine in (True, False):
            if mine and j == 0:
                continue
            copy = pltpu.make_async_remote_copy(
                src_ref=send_ref.at[kind if mine else 1 - kind, rem(e + j, count)],
                dst_ref=recv_ref.at[slot],
                send_sem=send_sem.at[2 * j + (0 if mine else 1)],
                recv_sem=recv_sem.at[slot],
                device_id=target(j, mine),
                device_id_type=MESH,
            )
            copy.start()
            copies.append(copy)
    local.wait()
    for j in range(count):
        for mine in (True, False):
            if mine and j == 0:
                continue
            source = rem(x if mine else other, 2) * count + rem(e + j, count)
            pltpu.make_async_remote_copy(
                src_ref=recv_ref.at[source],
                dst_ref=recv_ref.at[source],
                send_sem=send_sem.at[2 * j + (0 if mine else 1)],
                recv_sem=recv_sem.at[source],
                device_id=target(j, mine),
                device_id_type=MESH,
            ).wait_recv()
    for copy in copies:
        copy.wait_send()


def dispatch(send, count):
    shape = send.shape[2:]
    return pl.pallas_call(
        functools.partial(dispatch_kernel, count),
        out_shape=jax.ShapeDtypeStruct((2 * count,) + shape, send.dtype),
        in_specs=[pl.BlockSpec(memory_space=pltpu.VMEM)],
        out_specs=pl.BlockSpec(memory_space=pltpu.VMEM),
        scratch_shapes=[
            pltpu.SemaphoreType.DMA((2 * count,)),
            pltpu.SemaphoreType.DMA((2 * count,)),
            pltpu.SemaphoreType.DMA,
        ],
        compiler_params=pltpu.CompilerParams(
            collective_id=0, has_side_effects=True, vmem_limit_bytes=16 << 20
        ),
        name="dispatch",
    )(send)


def giveback_kernel(count, send_ref, recv_ref, send_sem, recv_sem, own_sem):
    z, e, x = lax.axis_index("seq"), lax.axis_index("expert"), lax.axis_index("mp")
    other = x + 1 - 2 * rem(x, 2)
    kind = rem(x + z, 2)

    def target(j, mine):
        return {"seq": z, "expert": rem(e + j, count), "mp": x if mine else other}

    barrier = pltpu.get_barrier_semaphore()
    for j in range(count):
        if j:
            pl.semaphore_signal(barrier, inc=1, device_id=target(j, True), device_id_type=MESH)
        pl.semaphore_signal(barrier, inc=1, device_id=target(j, False), device_id_type=MESH)
    pl.semaphore_wait(barrier, 2 * count - 1)

    local = pltpu.make_async_copy(send_ref.at[rem(x, 2) * count + e], recv_ref.at[kind, e], own_sem)
    local.start()
    copies = []
    for j in range(count):
        for mine in (True, False):
            if mine and j == 0:
                continue
            copy = pltpu.make_async_remote_copy(
                src_ref=send_ref.at[rem(x if mine else other, 2) * count + rem(e + j, count)],
                dst_ref=recv_ref.at[kind, e],
                send_sem=send_sem.at[2 * j + (0 if mine else 1)],
                recv_sem=recv_sem.at[kind * count + e],
                device_id=target(j, mine),
                device_id_type=MESH,
            )
            copy.start()
            copies.append(copy)
    local.wait()
    for j in range(count):
        for mine in (True, False):
            if mine and j == 0:
                continue
            half = kind if mine else 1 - kind
            source = rem(e + j, count)
            pltpu.make_async_remote_copy(
                src_ref=recv_ref.at[half, source],
                dst_ref=recv_ref.at[half, source],
                send_sem=send_sem.at[2 * j + (0 if mine else 1)],
                recv_sem=recv_sem.at[half * count + source],
                device_id=target(j, mine),
                device_id_type=MESH,
            ).wait_recv()
    for copy in copies:
        copy.wait_send()


def giveback(send, count):
    shape = send.shape[1:]
    return pl.pallas_call(
        functools.partial(giveback_kernel, count),
        out_shape=jax.ShapeDtypeStruct((2, count) + shape, send.dtype),
        in_specs=[pl.BlockSpec(memory_space=pltpu.VMEM)],
        out_specs=pl.BlockSpec(memory_space=pltpu.VMEM),
        scratch_shapes=[
            pltpu.SemaphoreType.DMA((2 * count,)),
            pltpu.SemaphoreType.DMA((2 * count,)),
            pltpu.SemaphoreType.DMA,
        ],
        compiler_params=pltpu.CompilerParams(
            collective_id=1, has_side_effects=True, vmem_limit_bytes=16 << 20
        ),
        name="giveback",
    )(send)


def dot_nt(a, b, **kwargs):
    return lax.dot_general(a, b, (((1,), (1,)), ((), ())), preferred_element_type=F32, **kwargs)


def experts_kernel(
    own_ref, wg_hbm, wu_hbm, wd_hbm, out_ref, dot_ref,
    xs, running, first, local, acc_t, acc_g, grads, dots, dot_slots, wg, wu, wd,
    w_sem, ag_send, ag_recv, rs_send, rs_recv, dot_send, dot_recv,
):
    rows, quarter = own_ref.shape[1], own_ref.shape[2]
    hidden = wg.shape[1]
    part = quarter // 2
    half = 4 * part
    z, x = lax.axis_index("seq"), lax.axis_index("mp")
    spot = [place(c, z, x) for c in range(2)]
    after = [coords(c, rem(spot[c] + 1, RING)) for c in range(2)]
    before = [coords(c, rem(spot[c] + RING - 1, RING)) for c in range(2)]
    to = [peer(*after[0]), peer(*before[0]), peer(*after[1]), peer(*before[1])]

    loads = [
        pltpu.make_async_copy(wg_hbm.at[0], wg, w_sem.at[0]),
        pltpu.make_async_copy(wu_hbm.at[0], wu, w_sem.at[1]),
    ]
    for r in range(4):
        loads.append(pltpu.make_async_copy(wd_hbm.at[0, :, pl.ds(r * quarter, quarter)], wd.at[r], w_sem.at[2 + r]))

    barrier = pltpu.get_barrier_semaphore()
    for r in range(4):
        pl.semaphore_signal(barrier, inc=1, device_id=to[r], device_id_type=MESH)
    for r in range(4):
        xs[r, spot[r // 2]] = own_ref[r]
    pl.semaphore_wait(barrier, 4)

    def held(r, s):
        c = r // 2
        return rem(spot[c] + RING - s, RING) if r % 2 == 0 else rem(spot[c] + s, RING)

    def gather(r, s, slot_step):
        block = xs.at[r, held(r, slot_step)]
        return pltpu.make_async_remote_copy(
            src_ref=block, dst_ref=block, send_sem=ag_send.at[r, s], recv_sem=ag_recv.at[r, s],
            device_id=to[r], device_id_type=MESH,
        )

    for r in range(4):
        gather(r, 1, 0).start()
    for load in loads:
        load.start()
    acc_t[...] = jnp.zeros_like(acc_t)
    acc_g[...] = jnp.zeros_like(acc_g)
    for load in loads:
        load.wait()

    def forward_unit(unit):
        b = div(unit, 8)
        r = div(rem(unit, 8), 2)
        kind = rem(unit, 2)
        c, back = div(r, 2), rem(r, 2)
        p = spot[0] * (1 - c) + spot[1] * c
        begin = pl.multiple_of(r * quarter, quarter)

        @pl.when(kind == 0)
        def _():
            base = jnp.where(back == 0, div(p, 2) - GROUP * b - 3, div(p + 1, 2) + GROUP * b) + 32
            lhs = jnp.concatenate([xs[r, 2 * rem(base + i, 16)] for i in range(GROUP)], axis=0)
            gate = jnp.dot(lhs, wg[pl.ds(begin, quarter), :], preferred_element_type=F32)
            up = jnp.dot(lhs, wu[pl.ds(begin, quarter), :], preferred_element_type=F32)
            for i in range(GROUP):
                t = rem(base + i, 16)
                acc_t[c, t, :, :hidden] += gate[i * rows:(i + 1) * rows]
                acc_t[c, t, :, hidden:] += up[i * rows:(i + 1) * rows]

        @pl.when(kind == 1)
        def _():
            base = jnp.where(back == 0, div(p + 1, 2) - 1 - GROUP * b - 3, div(p, 2) + GROUP * b) + 32
            lhs = jnp.concatenate([xs[r, 2 * rem(base + i, 16) + 1] for i in range(GROUP)], axis=0)
            grad = dot_nt(lhs, wd[r])
            for i in range(GROUP):
                acc_g[c, rem(base + i, 16)] += grad[i * rows:(i + 1) * rows]

    def ag_step(s, carry):
        for r in range(4):
            gather(r, s, s).wait_recv()

            @pl.when(s < RING - 1)
            def _():
                gather(r, s + 1, s).start()

        @pl.when(s >= SPAN)
        def _():
            forward_unit(s - SPAN)

        return carry

    lax.fori_loop(1, RING, ag_step, 0)

    def tail_unit(u, carry):
        forward_unit(u + 3 * SPAN)
        return carry

    lax.fori_loop(0, SPAN, tail_unit, 0)

    ones = jnp.ones((8, 128), F32)
    for pair in range(16):
        pz, px = pair // 2, 2 * (pair % 2)
        holders = [(pz, px), (pz, px + 1)]
        if (px + pz) % 2:
            holders = holders[::-1]
        t = [place(c, *holders[0]) // 2 for c in range(2)]
        g = [place(c, *holders[1]) // 2 for c in range(2)]
        pre_gate = acc_t[0, t[0], :, :hidden] + acc_t[1, t[1], :, :hidden]
        pre_up = acc_t[0, t[0], :, hidden:] + acc_t[1, t[1], :, hidden:]
        grad_hidden = acc_g[0, g[0]] + acc_g[1, g[1]]
        sigma = jax.nn.sigmoid(pre_gate)
        act = pre_gate * sigma
        inner = grad_hidden * act * pre_up
        grad_gate = (grad_hidden * pre_up * sigma * (1.0 + pre_gate * (1.0 - sigma))).astype(BF)
        grad_up = (grad_hidden * act).astype(BF)
        for c in range(2):
            for q in (2 * t[c], 2 * g[c] + 1):
                grads[c, q, :, :hidden] = grad_gate
                grads[c, q, :, hidden:] = grad_up
        folded = inner[:, 0:128]
        for i in range(1, hidden // 128):
            folded = folded + inner[:, i * 128:(i + 1) * 128]
        sums = dot_nt(ones, folded, precision=lax.Precision.HIGHEST)
        for q in (2 * t[0], 2 * g[0] + 1):
            dots[q, :, :rows] = sums

    def backward_unit(unit):
        b = div(unit, 8)
        r = div(rem(unit, 8), 2)
        kind = rem(unit, 2)
        c, back = div(r, 2), rem(r, 2)
        p = spot[0] * (1 - c) + spot[1] * c
        j0 = rem(p + 1 + kind, 2)
        steps = [SPAN * b + j0 + 2 * i for i in range(GROUP)]
        where = [jnp.where(back == 0, rem(p + 2 * RING - 1 - s, RING), rem(p + 1 + s, RING)) for s in steps]
        lhs = jnp.concatenate([grads[c, q] for q in where], axis=0)
        begin = pl.multiple_of(kind * half + r * part, part)
        y = dot_nt(lhs[:, :hidden], wg[pl.ds(begin, part), :]) + dot_nt(lhs[:, hidden:], wu[pl.ds(begin, part), :])
        for i in range(GROUP):
            local[r, rem(steps[i], 2 * SPAN)] = y[i * rows:(i + 1) * rows].astype(local.dtype)

    def head_unit(u, carry):
        backward_unit(u)
        return carry

    lax.fori_loop(0, SPAN, head_unit, 0)

    def scatter(r, s, src):
        return pltpu.make_async_remote_copy(
            src_ref=src, dst_ref=running.at[r, s], send_sem=rs_send.at[r, s], recv_sem=rs_recv.at[r, s],
            device_id=to[r], device_id_type=MESH,
        )

    def dot_copy(s, src):
        return pltpu.make_async_remote_copy(
            src_ref=src, dst_ref=dot_slots.at[s], send_sem=dot_send.at[s], recv_sem=dot_recv.at[s],
            device_id=to[0], device_id_type=MESH,
        )

    def dest(s):
        return rem(spot[0] + 2 * RING - 1 - s, RING)

    for r in range(4):
        first[r] = local[r, 0].astype(BF)
        scatter(r, 0, first.at[r]).start()
    dot_copy(0, dots.at[dest(0)]).start()
    backward_unit(jnp.int32(SPAN))

    def rs_step(s, carry):
        for r in range(4):
            scatter(r, s - 1, running.at[r, s - 1]).wait_recv()
            total = running[r, s - 1].astype(F32) + local[r, rem(s, 2 * SPAN)].astype(F32)
            running[r, s - 1] = total.astype(BF)
            scatter(r, s, running.at[r, s - 1]).start()
        dot_copy(s - 1, dot_slots.at[s - 1]).wait_recv()
        dot_slots[s - 1] = dot_slots[s - 1] + dots[dest(s)]
        dot_copy(s, dot_slots.at[s - 1]).start()

        @pl.when(s < 3 * SPAN)
        def _():
            backward_unit(s + SPAN)

        return carry

    lax.fori_loop(1, RING - 1, rs_step, 0)
    last = RING - 2
    for r in range(4):
        scatter(r, last, running.at[r, last]).wait_recv()
        out_ref[r] = (running[r, last].astype(F32) + local[r, (RING - 1) % (2 * SPAN)].astype(F32)).astype(BF)
    dot_copy(last, dot_slots.at[last]).wait_recv()
    dot_ref[...] = dot_slots[last] + dots[dest(RING - 1)]

    def drain(s, carry):
        for r in range(4):
            gather(r, s + 1, s).wait_send()
            scatter(r, s, running.at[r, s]).wait_send()
        dot_copy(s, dot_slots.at[s]).wait_send()
        return carry

    lax.fori_loop(0, RING - 1, drain, 0)


def run_experts(own, gate_weight, up_weight, down_weight):
    rows, quarter = own.shape[1:]
    width, hidden = gate_weight.shape[1:]
    part = quarter // 2
    vmem = pl.BlockSpec(memory_space=pltpu.VMEM)
    hbm = pl.BlockSpec(memory_space=pl.ANY)
    return pl.pallas_call(
        experts_kernel,
        out_shape=(
            jax.ShapeDtypeStruct((4, rows, part), BF),
            jax.ShapeDtypeStruct((8, 128), F32),
        ),
        in_specs=[vmem, hbm, hbm, hbm],
        out_specs=(vmem, vmem),
        scratch_shapes=[
            pltpu.VMEM((4, RING, rows, quarter), BF),
            pltpu.VMEM((4, RING - 1, rows, part), BF),
            pltpu.VMEM((4, rows, part), BF),
            pltpu.VMEM((4, 2 * SPAN, rows, part), BF),
            pltpu.VMEM((2, 16, rows, 2 * hidden), F32),
            pltpu.VMEM((2, 16, rows, hidden), F32),
            pltpu.VMEM((2, RING, rows, 2 * hidden), BF),
            pltpu.VMEM((RING, 8, 128), F32),
            pltpu.VMEM((RING, 8, 128), F32),
            pltpu.VMEM((width, hidden), BF),
            pltpu.VMEM((width, hidden), BF),
            pltpu.VMEM((4, hidden, quarter), BF),
            pltpu.SemaphoreType.DMA((6,)),
            pltpu.SemaphoreType.DMA((4, RING)),
            pltpu.SemaphoreType.DMA((4, RING)),
            pltpu.SemaphoreType.DMA((4, RING)),
            pltpu.SemaphoreType.DMA((4, RING)),
            pltpu.SemaphoreType.DMA((RING,)),
            pltpu.SemaphoreType.DMA((RING,)),
        ],
        compiler_params=pltpu.CompilerParams(
            collective_id=2, has_side_effects=True, vmem_limit_bytes=62 << 20
        ),
        name="experts",
    )(own, gate_weight, up_weight, down_weight)


def on_device(tokens, out_grad, kept_mask, routes, router, gate_weight, up_weight, down_weight):
    row_count, width = tokens.shape
    count = lax.axis_size("expert")
    capacity = 3 * row_count // 8
    columns = lax.broadcasted_iota(jnp.int32, (row_count, count), 1)
    first_hot = (routes[:, 0:1] == columns).astype(F32)
    second_hot = (routes[:, 1:2] == columns).astype(F32)
    keep_rows = kept_mask.astype(F32)
    chosen = ((first_hot + second_hot) * keep_rows[:, None]).astype(jnp.int32)
    position = jnp.cumsum(chosen, axis=0) - 1
    slot_iota = lax.broadcasted_iota(jnp.int32, (row_count, count, capacity), 2)
    select_mask = (chosen[:, :, None] == 1) & (position[:, :, None] == slot_iota)
    select_bf = select_mask.astype(BF)
    select_full = select_mask.astype(F32)
    both = jnp.stack([tokens, out_grad])
    send = jnp.einsum("tec,ktd->kecd", select_bf, both, preferred_element_type=F32).astype(BF)
    got = dispatch(send, count)
    own = got.reshape(2 * count * capacity, 4, width // 4).transpose(1, 0, 2)
    sums, dot_sums = run_experts(own, gate_weight, up_weight, down_weight)
    sums = sums.transpose(1, 0, 2).reshape(2 * count, capacity, width // 2)

    dot_rows = dot_sums[0, : 2 * count * capacity].reshape(2 * count, capacity, 1)
    top = lax.reduce_precision(dot_rows, 8, 7)
    middle = lax.reduce_precision(dot_rows - top, 8, 7)
    low = lax.reduce_precision(dot_rows - top - middle, 8, 7)
    extra = jnp.concatenate([top, middle, low], axis=2).astype(BF)
    extra = jnp.pad(extra, ((0, 0), (0, 0), (0, 125)))
    back = giveback(jnp.concatenate([sums, extra], axis=2), count)

    logits = jnp.dot(tokens, router, preferred_element_type=F32)
    first_logit = jnp.sum(logits * first_hot, axis=1)
    second_logit = jnp.sum(logits * second_hot, axis=1)
    gate_first = jax.nn.sigmoid(first_logit - second_logit)
    gate_second = jax.nn.sigmoid(second_logit - first_logit)
    gate_table = (first_hot * gate_first[:, None] + second_hot * gate_second[:, None]).astype(BF)
    weigh = select_bf * gate_table[:, :, None]
    expert_sum = jnp.einsum("tec,kecd->tkd", weigh, back[..., : width // 2], preferred_element_type=F32)
    expert_sum = expert_sum.reshape(row_count, width)
    dot_parts = back[0, :, :, width // 2 : width // 2 + 3].astype(F32)
    dot_back = dot_parts[..., 0] + dot_parts[..., 1] + dot_parts[..., 2]
    dot_table = jnp.sum(select_full * dot_back[None], axis=2)
    dot_first = jnp.sum(dot_table * first_hot, axis=1)
    dot_second = jnp.sum(dot_table * second_hot, axis=1)
    product = gate_first * gate_second * keep_rows
    grad_first = product * (dot_first - dot_second)
    grad_second = product * (dot_second - dot_first)
    logit_grad = first_hot * grad_first[:, None] + second_hot * grad_second[:, None]
    router_term = jnp.dot(logit_grad, router.astype(F32).T, precision=lax.Precision.HIGHEST)
    d_tokens = ((expert_sum + router_term) * keep_rows[:, None]).astype(BF)
    gate_grad = jnp.stack([grad_first, grad_second], axis=1)
    return (d_tokens, gate_grad)


def solution(mesh):
    return jax.shard_map(
        on_device,
        mesh=mesh,
        in_specs=(
            P(("seq", "expert", "mp"), None),
            P(("seq", "expert", "mp"), None),
            P(("seq", "expert", "mp")),
            P(("seq", "expert", "mp"), None),
            P(),
            P("expert", None, ("seq", "mp")),
            P("expert", None, ("seq", "mp")),
            P("expert", ("seq", "mp"), None),
        ),
        out_specs=(P(("seq", "expert", "mp"), None), P(("seq", "expert", "mp"), None)),
        check_vma=False,
    )
```

time: 690 us -> 338 us (0.49)
  waiting for transfers between devices: 384 us -> 0 us
  Pallas kernels: 0 us -> 327 us
  blocking collectives: 144 us -> 0 us
  local copies, waits for them, and re-layouts: 84.8 us -> 5.94 us
  matrix products: 48.3 us -> 2.74 us
  between operations: 14.5 us -> 0.78 us
  starting transfers between devices: 9.09 us -> 0 us
    pallas_call x0 -> x3, Pallas kernels: none -> 327 us  [the longest x1 257 us: run_experts(): pl.pallas_call(experts_kernel, out_shape=(jax.ShapeDtypeStruct((4, rows,...]
    reduce_scatter x1 -> x0, waiting for transfers between devices: 236 us -> none  [on_device(): lax.psum_scatter(expert_grad.astype(jnp.bfloat16), ('seq', 'mp'), scatter...]
    all_gather x2 -> x0, waiting for transfers between devices: 142 us -> none  [the longest x1 88.6 us: on_device(): lax.all_gather(token_recv, ('seq', 'mp'), axis=0, tiled=True)]
    unnamed x1 -> x0, blocking collectives: 57.6 us -> none
    all_to_all x4 -> x0, blocking collectives: 56.2 us -> none  [the longest x1 23.4 us: on_device(): lax.all_to_all(dot_own.reshape(expert_count, capacity).astype(jnp.bfloat1...]
    dot_general x10 -> x4, matrix products: 48.3 us -> 2.74 us  [the longest x1 1.29 us: on_device(): jnp.einsum('tec,ktd->kecd', select_bf, both, preferred_element_type=F32)]
    reshape x2 -> x3, local copies, waits for them, and re-layouts: 47.1 us -> 1.74 us  [the longest x2 1.62 us: on_device(): own = got.reshape(2 * count * capacity, 4, width // 4).transpose(1, 0, 2)]
    all_gather x1 -> x0, blocking collectives: 30.7 us -> none  [on_device(): lax.all_gather(gate_recv, ('seq', 'mp'), axis=0, tiled=True)]
  transfers between devices with their start and end apart: 4 -> 0, of which waited for: 4 -> 0; matrix products, arithmetic and copies ran while one was open for 8% -> 0% of each run, Pallas kernels for 0% -> 0%
where the time goes in v1:
time: 338 us
  Pallas kernels  327 us (97%)
  local copies, waits for them, and re-layouts  5.94 us (2%)
    pallas_call x1, Pallas kernels, run_experts(): pl.pallas_call(experts_kernel, out_shape=(jax.ShapeDtypeStruct((4, rows,...  257 us
    pallas_call x1, Pallas kernels, giveback(): pl.pallas_call(functools.partial(giveback_kernel, count), out_shape=jax.S...  54 us
    pallas_call x1, Pallas kernels, dispatch(): pl.pallas_call(functools.partial(dispatch_kernel, count), out_shape=jax.S...  16.3 us

profile of v1, /device:TPU:1, one launch (start us, length us, event | category | flops | bytes accessed | tf_op | source)
XLA Modules:
  0.0 338.1 jit_solution(17794866700103893305)
XLA Ops:
  0.6 0.0 copy-start
  0.6 0.7 convert_element_type.65
  1.3 0.8 slice_bitcast_fusion.1
  2.1 0.1 copy.59
  2.2 0.2 reduce_window_sum.11
  2.4 0.1 copy.60
  2.4 1.3 convolution_convert_fusion
  3.7 0.5 copy.86
  4.3 16.3 %dispatch.1 = bf16[16,3,6144]{2,1,0:T(4,128)(2,1)S(1)} custom-call(bf16[2,8,3,6144]{3,2,1,0:T(4,128)(2,1)S(1)} %bitcast.37), custom_call_target="tpu_custom_call" | custom-call | tf_op jit(solution)/shard_map/dispatch/pallas_call | solution.py:97
  20.6 0.7 reshape.287
  21.3 0.9 copy.87
  22.2 256.6 %experts.1 = (bf16[4,48,768]{2,1,0:T(8,128)(2,1)}, f32[8,128]{1,0:T(8,128)}) custom-call(bf16[4,48,1536]{2,1,0:T(8,128)(2,1)} %bitcast.38, bf16[1,6144,256]{2,1,0:T(8,128)(2,1)} %wg_hbm.1, bf16[1,6144,256]{2,1,0:T(8,128)(2,1)} %wu_hbm.1, bf16[1,256,6144]{2,1,0:T(8,128)(2,1)} %wd_hbm.1), custom_call_target="tpu_custom_call" | custom-call | tf_op jit(solution)/shard_map/experts/pallas_call | solution.py:395
  278.8 0.0 copy-start.1
  278.8 0.0 copy-start.2
  278.8 1.2 copy.65
  280.0 0.7 slice_reduce_fusion
  280.7 0.1 reshape_squeeze.3
  280.8 0.2 copy.68
  281.0 0.2 copy.67
  281.2 0.1 fusion.12
  281.3 0.1 reshape.288
  281.4 0.2 pad_maximum_fusion.send_ref
  281.6 54.0 %giveback.1 = bf16[2,8,3,3200]{3,2,1,0:T(4,128)(2,1)S(1)} custom-call(bf16[16,3,3200]{2,1,0:T(4,128)(2,1)S(1)} %pad_maximum_fusion.send_ref), custom_call_target="tpu_custom_call" | custom-call | tf_op jit(solution)/shard_map/giveback/pallas_call | solution.py:167
  335.6 0.1 slice.33
  335.8 0.1 copy.71
  335.9 0.1 copy.72
  336.0 0.2 select_reduce_fusion.4
  336.2 0.0 copy-done.2
  336.2 0.6 pad_maximum_fusion.1
  336.8 0.1 copy.61
  336.9 0.3 fusion.2
  337.2 0.9 fusion.1
  (14 shorter events, 0.1 us)
Async XLA Ops:
  0.6 335.4 %copy-start = (bf16[6144,8]{0,1:T(8,128)(2,1)S(1)}, bf16[6144,8]{0,1:T(8,128)(2,1)}, u32[]{:S(2)}) copy-start(bf16[6144,8]{0,1:T(8,128)(2,1)} %param.12) | copy-start | bytes 294916
  278.8 57.2 %copy-start.1 = (bf16[8,6144]{1,0:T(8,128)(2,1)S(1)}, bf16[8,6144]{1,0:T(8,128)(2,1)}, u32[]{:S(2)}) copy-start(bf16[8,6144]{1,0:T(8,128)(2,1)} %param.8) | copy-start | bytes 294916
  278.8 57.4 %copy-start.2 = (s32[8]{0:T(128)S(1)}, s32[8]{0:T(128)}, u32[]{:S(2)}) copy-start(s32[8]{0:T(128)} %param.10) | copy-start | bytes 100

commit v2 on v1

--- a/solution.py
+++ b/solution.py
@@ -11,8 +11,9 @@
 BF = jnp.bfloat16
 F32 = jnp.float32
 RING = 32
+HOPS = 16
 GROUP = 4
-SPAN = 8
+CHUNK = 16
 
 
 def div(a, b):
@@ -187,13 +188,13 @@
 
 def experts_kernel(
     own_ref, wg_hbm, wu_hbm, wd_hbm, out_ref, dot_ref,
-    xs, running, first, local, acc_t, acc_g, grads, dots, dot_slots, wg, wu, wd,
+    xs, running, local, acc_t, acc_g, grads, dots, dot_slots, wg, wu, wd,
     w_sem, ag_send, ag_recv, rs_send, rs_recv, dot_send, dot_recv,
 ):
-    rows, quarter = own_ref.shape[1], own_ref.shape[2]
+    rows, share = own_ref.shape[1], own_ref.shape[2]
     hidden = wg.shape[1]
-    part = quarter // 2
-    half = 4 * part
+    part = share // 2
+    half = 2 * part
     z, x = lax.axis_index("seq"), lax.axis_index("mp")
     spot = [place(c, z, x) for c in range(2)]
     after = [coords(c, rem(spot[c] + 1, RING)) for c in range(2)]
@@ -204,84 +205,98 @@
         pltpu.make_async_copy(wg_hbm.at[0], wg, w_sem.at[0]),
         pltpu.make_async_copy(wu_hbm.at[0], wu, w_sem.at[1]),
     ]
-    for r in range(4):
-        loads.append(pltpu.make_async_copy(wd_hbm.at[0, :, pl.ds(r * quarter, quarter)], wd.at[r], w_sem.at[2 + r]))
+    for c in range(2):
+        loads.append(pltpu.make_async_copy(wd_hbm.at[0, :, pl.ds(c * share, share)], wd.at[c], w_sem.at[2 + c]))
 
     barrier = pltpu.get_barrier_semaphore()
     for r in range(4):
         pl.semaphore_signal(barrier, inc=1, device_id=to[r], device_id_type=MESH)
-    for r in range(4):
-        xs[r, spot[r // 2]] = own_ref[r]
+    for c in range(2):
+        xs[c, spot[c]] = own_ref[c]
     pl.semaphore_wait(barrier, 4)
 
     def held(r, s):
         c = r // 2
         return rem(spot[c] + RING - s, RING) if r % 2 == 0 else rem(spot[c] + s, RING)
 
-    def gather(r, s, slot_step):
-        block = xs.at[r, held(r, slot_step)]
+    def gather(r, s, k, where, halved=False):
+        lanes = pl.ds((r % 2) * part, part) if halved else slice(None)
+        block = xs.at[r // 2, where, pl.ds(k * CHUNK, CHUNK), lanes]
         return pltpu.make_async_remote_copy(
-            src_ref=block, dst_ref=block, send_sem=ag_send.at[r, s], recv_sem=ag_recv.at[r, s],
+            src_ref=block, dst_ref=block, send_sem=ag_send.at[r, s, k], recv_sem=ag_recv.at[r, s, k],
             device_id=to[r], device_id_type=MESH,
         )
 
-    for r in range(4):
-        gather(r, 1, 0).start()
+    chunks = rows // CHUNK
+    for k in range(chunks):
+        for r in range(4):
+            gather(r, 1, k, spot[r // 2]).start()
     for load in loads:
         load.start()
-    acc_t[...] = jnp.zeros_like(acc_t)
-    acc_g[...] = jnp.zeros_like(acc_g)
     for load in loads:
         load.wait()
 
     def forward_unit(unit):
-        b = div(unit, 8)
-        r = div(rem(unit, 8), 2)
+        b = div(unit, 4)
+        c = div(rem(unit, 4), 2)
         kind = rem(unit, 2)
-        c, back = div(r, 2), rem(r, 2)
         p = spot[0] * (1 - c) + spot[1] * c
-        begin = pl.multiple_of(r * quarter, quarter)
+        begin = pl.multiple_of(c * share, share)
+
+        def positions(parity):
+            low = p - GROUP * (b + 1)
+            low = low + rem(low + parity + 2 * RING, 2) + RING
+            high = p + GROUP * b
+            high = high + rem(high + parity, 2)
+            return [div(rem(q, RING), 2) for q in (low, low + 2, high, high + 2)]
 
         @pl.when(kind == 0)
         def _():
-            base = jnp.where(back == 0, div(p, 2) - GROUP * b - 3, div(p + 1, 2) + GROUP * b) + 32
-            lhs = jnp.concatenate([xs[r, 2 * rem(base + i, 16)] for i in range(GROUP)], axis=0)
-            gate = jnp.dot(lhs, wg[pl.ds(begin, quarter), :], preferred_element_type=F32)
-            up = jnp.dot(lhs, wu[pl.ds(begin, quarter), :], preferred_element_type=F32)
-            for i in range(GROUP):
-                t = rem(base + i, 16)
-                acc_t[c, t, :, :hidden] += gate[i * rows:(i + 1) * rows]
-                acc_t[c, t, :, hidden:] += up[i * rows:(i + 1) * rows]
+            where = positions(0)
+            lhs = jnp.concatenate([xs[c, 2 * t] for t in where], axis=0)
+            gate = jnp.dot(lhs, wg[pl.ds(begin, share), :], preferred_element_type=F32)
+            up = jnp.dot(lhs, wu[pl.ds(begin, share), :], preferred_element_type=F32)
+            for i, t in enumerate(where):
+                acc_t[c, t, :, :hidden] = gate[i * rows:(i + 1) * rows]
+                acc_t[c, t, :, hidden:] = up[i * rows:(i + 1) * rows]
 
         @pl.when(kind == 1)
         def _():
-            base = jnp.where(back == 0, div(p + 1, 2) - 1 - GROUP * b - 3, div(p, 2) + GROUP * b) + 32
-            lhs = jnp.concatenate([xs[r, 2 * rem(base + i, 16) + 1] for i in range(GROUP)], axis=0)
-            grad = dot_nt(lhs, wd[r])
-            for i in range(GROUP):
-                acc_g[c, rem(base + i, 16)] += grad[i * rows:(i + 1) * rows]
+            where = positions(1)
+            lhs = jnp.concatenate([xs[c, 2 * t + 1] for t in where], axis=0)
+            grad = dot_nt(lhs, wd[c])
+            for i, t in enumerate(where):
+                acc_g[c, t] = grad[i * rows:(i + 1) * rows]
 
     def ag_step(s, carry):
+        for k in range(chunks):
+            for r in range(4):
+                gather(r, s, k, held(r, s)).wait_recv()
+
+                @pl.when(s < HOPS - 1)
+                def _():
+                    gather(r, s + 1, k, held(r, s)).start()
+
+                @pl.when(s == HOPS - 1)
+                def _():
+                    gather(r, s + 1, k, held(r, s), True).start()
+
+        @pl.when(s >= GROUP)
+        def _():
+            forward_unit(s - GROUP)
+
+        return carry
+
+    lax.fori_loop(1, HOPS, ag_step, 0)
+    for k in range(chunks):
         for r in range(4):
-            gather(r, s, s).wait_recv()
-
-            @pl.when(s < RING - 1)
-            def _():
-                gather(r, s + 1, s).start()
-
-        @pl.when(s >= SPAN)
-        def _():
-            forward_unit(s - SPAN)
-
+            gather(r, HOPS, k, held(r, HOPS), True).wait_recv()
+
+    def tail_unit(u, carry):
+        forward_unit(u)
         return carry
 
-    lax.fori_loop(1, RING, ag_step, 0)
-
-    def tail_unit(u, carry):
-        forward_unit(u + 3 * SPAN)
-        return carry
-
-    lax.fori_loop(0, SPAN, tail_unit, 0)
+    lax.fori_loop(HOPS - GROUP, HOPS, tail_unit, 0)
 
     ones = jnp.ones((8, 128), F32)
     for pair in range(16):
@@ -310,116 +325,160 @@
         for q in (2 * t[0], 2 * g[0] + 1):
             dots[q, :, :rows] = sums
 
+    def dest(r, s):
+        c = r // 2
+        return rem(spot[c] + HOPS + RING - s, RING) if r % 2 == 0 else rem(spot[c] + HOPS + s, RING)
+
     def backward_unit(unit):
-        b = div(unit, 8)
-        r = div(rem(unit, 8), 2)
+        b = div(unit, 4)
+        c = div(rem(unit, 4), 2)
         kind = rem(unit, 2)
-        c, back = div(r, 2), rem(r, 2)
         p = spot[0] * (1 - c) + spot[1] * c
-        j0 = rem(p + 1 + kind, 2)
-        steps = [SPAN * b + j0 + 2 * i for i in range(GROUP)]
-        where = [jnp.where(back == 0, rem(p + 2 * RING - 1 - s, RING), rem(p + 1 + s, RING)) for s in steps]
+        low = p + HOPS + RING - GROUP * b - (GROUP - 1)
+        low = low + rem(low + kind, 2)
+        high = p + HOPS + GROUP * b + 1
+        high = high + rem(high + kind, 2)
+        where = [2 * div(rem(q, RING), 2) + kind for q in (low, low + 2, high, high + 2)]
         lhs = jnp.concatenate([grads[c, q] for q in where], axis=0)
-        begin = pl.multiple_of(kind * half + r * part, part)
+        begin = pl.multiple_of(kind * half + c * part, part)
         y = dot_nt(lhs[:, :hidden], wg[pl.ds(begin, part), :]) + dot_nt(lhs[:, hidden:], wu[pl.ds(begin, part), :])
         for i in range(GROUP):
-            local[r, rem(steps[i], 2 * SPAN)] = y[i * rows:(i + 1) * rows].astype(local.dtype)
+            local[c, where[i]] = y[i * rows:(i + 1) * rows].astype(local.dtype)
 
     def head_unit(u, carry):
         backward_unit(u)
         return carry
 
-    lax.fori_loop(0, SPAN, head_unit, 0)
-
-    def scatter(r, s, src):
+    lax.fori_loop(0, GROUP, head_unit, 0)
+
+    def scatter(r, s, k):
+        cut = pl.ds(k * CHUNK, CHUNK)
         return pltpu.make_async_remote_copy(
-            src_ref=src, dst_ref=running.at[r, s], send_sem=rs_send.at[r, s], recv_sem=rs_recv.at[r, s],
+            src_ref=running.at[r, s - 1, cut], dst_ref=running.at[r, s, cut],
+            send_sem=rs_send.at[r, s, k], recv_sem=rs_recv.at[r, s, k],
             device_id=to[r], device_id_type=MESH,
         )
 
-    def dot_copy(s, src):
+    def scatter_first(r, k):
+        cut, lanes = pl.ds(k * CHUNK, CHUNK), pl.ds((r % 2) * (part // 2), part // 2)
         return pltpu.make_async_remote_copy(
-            src_ref=src, dst_ref=dot_slots.at[s], send_sem=dot_send.at[s], recv_sem=dot_recv.at[s],
-            device_id=to[0], device_id_type=MESH,
+            src_ref=local.at[r // 2, dest(r, 0), cut, lanes], dst_ref=running.at[r, 0, cut, lanes],
+            send_sem=rs_send.at[r, 0, k], recv_sem=rs_recv.at[r, 0, k],
+            device_id=to[r], device_id_type=MESH,
         )
 
-    def dest(s):
-        return rem(spot[0] + 2 * RING - 1 - s, RING)
-
-    for r in range(4):
-        first[r] = local[r, 0].astype(BF)
-        scatter(r, 0, first.at[r]).start()
-    dot_copy(0, dots.at[dest(0)]).start()
-    backward_unit(jnp.int32(SPAN))
+    def dot_copy(d, s, src):
+        return pltpu.make_async_remote_copy(
+            src_ref=src, dst_ref=dot_slots.at[d, s], send_sem=dot_send.at[d, s], recv_sem=dot_recv.at[d, s],
+            device_id=to[d], device_id_type=MESH,
+        )
+
+    for k in range(chunks):
+        for r in range(4):
+            scatter_first(r, k).start()
+    dot_copy(0, 0, dots.at[dest(0, 0)]).start()
+    backward_unit(jnp.int32(GROUP))
+
+    for k in range(chunks):
+        cut = slice(k * CHUNK, (k + 1) * CHUNK)
+        for r in range(4):
+            mine = slice((r % 2) * (part // 2), (r % 2 + 1) * (part // 2))
+            rest = slice((1 - r % 2) * (part // 2), (2 - r % 2) * (part // 2))
+            scatter_first(r, k).wait_recv()
+            total = running[r, 0, cut, mine].astype(F32) + local[r // 2, dest(r, 1), cut, mine].astype(F32)
+            running[r, 0, cut, mine] = total.astype(BF)
+            running[r, 0, cut, rest] = local[r // 2, dest(r, 1), cut, rest]
+            scatter(r, 1, k).start()
+    dot_copy(0, 0, dot_slots.at[0, 0]).wait_recv()
+    dot_slots[0, 0] = dot_slots[0, 0] + dots[dest(0, 1)]
+    dot_copy(0, 1, dot_slots.at[0, 0]).start()
+    dot_copy(1, 1, dots.at[dest(1, 1)]).start()
+    backward_unit(jnp.int32(GROUP + 1))
 
     def rs_step(s, carry):
+        for k in range(chunks):
+            cut = slice(k * CHUNK, (k + 1) * CHUNK)
+            for r in range(4):
+                scatter(r, s - 1, k).wait_recv()
+                total = running[r, s - 1, cut].astype(F32) + local[r // 2, dest(r, s), cut].astype(F32)
+                running[r, s - 1, cut] = total.astype(BF)
+                scatter(r, s, k).start()
+        for d in range(2):
+            dot_copy(d, s - 1, dot_slots.at[d, s - 1]).wait_recv()
+            dot_slots[d, s - 1] = dot_slots[d, s - 1] + dots[dest(d, s)]
+            dot_copy(d, s, dot_slots.at[d, s - 1]).start()
+
+        @pl.when(s < HOPS - GROUP)
+        def _():
+            backward_unit(s + GROUP)
+
+        return carry
+
+    lax.fori_loop(2, HOPS, rs_step, 0)
+    last = HOPS - 1
+    for k in range(chunks):
+        cut = slice(k * CHUNK, (k + 1) * CHUNK)
+        for c in range(2):
+            scatter(2 * c, last, k).wait_recv()
+            scatter(2 * c + 1, last, k).wait_recv()
+            both = running[2 * c, last, cut].astype(F32) + running[2 * c + 1, last, cut].astype(F32)
+            out_ref[c, cut] = (both + local[c, spot[c], cut].astype(F32)).astype(BF)
+    for d in range(2):
+        dot_copy(d, last, dot_slots.at[d, last]).wait_recv()
+    dot_ref[...] = dot_slots[0, last] + dot_slots[1, last] + dots[spot[0]]
+
+    for k in range(chunks):
         for r in range(4):
-            scatter(r, s - 1, running.at[r, s - 1]).wait_recv()
-            total = running[r, s - 1].astype(F32) + local[r, rem(s, 2 * SPAN)].astype(F32)
-            running[r, s - 1] = total.astype(BF)
-            scatter(r, s, running.at[r, s - 1]).start()
-        dot_copy(s - 1, dot_slots.at[s - 1]).wait_recv()
-        dot_slots[s - 1] = dot_slots[s - 1] + dots[dest(s)]
-        dot_copy(s, dot_slots.at[s - 1]).start()
-
-        @pl.when(s < 3 * SPAN)
-        def _():
-            backward_unit(s + SPAN)
-
+            gather(r, HOPS, k, held(r, HOPS - 1), True).wait_send()
+            scatter_first(r, k).wait_send()
+    dot_copy(0, 0, dots.at[dest(0, 0)]).wait_send()
+
+    def drain(s, carry):
+        for k in range(chunks):
+            for r in range(4):
+                gather(r, s, k, held(r, s - 1)).wait_send()
+                scatter(r, s, k).wait_send()
+        for d in range(2):
+            dot_copy(d, s, dot_slots.at[d, s - 1]).wait_send()
         return carry
 
-    lax.fori_loop(1, RING - 1, rs_step, 0)
-    last = RING - 2
-    for r in range(4):
-        scatter(r, last, running.at[r, last]).wait_recv()
-        out_ref[r] = (running[r, last].astype(F32) + local[r, (RING - 1) % (2 * SPAN)].astype(F32)).astype(BF)
-    dot_copy(last, dot_slots.at[last]).wait_recv()
-    dot_ref[...] = dot_slots[last] + dots[dest(RING - 1)]
-
-    def drain(s, carry):
-        for r in range(4):
-            gather(r, s + 1, s).wait_send()
-            scatter(r, s, running.at[r, s]).wait_send()
-        dot_copy(s, dot_slots.at[s]).wait_send()
-        return carry
-
-    lax.fori_loop(0, RING - 1, drain, 0)
+    lax.fori_loop(1, HOPS, drain, 0)
 
 
 def run_experts(own, gate_weight, up_weight, down_weight):
-    rows, quarter = own.shape[1:]
+    rows, share = own.shape[1:]
     width, hidden = gate_weight.shape[1:]
-    part = quarter // 2
+    part = share // 2
+    chunks = rows // CHUNK
     vmem = pl.BlockSpec(memory_space=pltpu.VMEM)
     hbm = pl.BlockSpec(memory_space=pl.ANY)
     return pl.pallas_call(
         experts_kernel,
         out_shape=(
-            jax.ShapeDtypeStruct((4, rows, part), BF),
+            jax.ShapeDtypeStruct((2, rows, part), BF),
             jax.ShapeDtypeStruct((8, 128), F32),
         ),
         in_specs=[vmem, hbm, hbm, hbm],
         out_specs=(vmem, vmem),
         scratch_shapes=[
-            pltpu.VMEM((4, RING, rows, quarter), BF),
-            pltpu.VMEM((4, RING - 1, rows, part), BF),
-            pltpu.VMEM((4, rows, part), BF),
-            pltpu.VMEM((4, 2 * SPAN, rows, part), BF),
+            pltpu.VMEM((2, RING, rows, share), BF),
+            pltpu.VMEM((4, HOPS, rows, part), BF),
+            pltpu.VMEM((2, RING, rows, part), BF),
             pltpu.VMEM((2, 16, rows, 2 * hidden), F32),
             pltpu.VMEM((2, 16, rows, hidden), F32),
             pltpu.VMEM((2, RING, rows, 2 * hidden), BF),
             pltpu.VMEM((RING, 8, 128), F32),
-            pltpu.VMEM((RING, 8, 128), F32),
+            pltpu.VMEM((2, HOPS, 8, 128), F32),
             pltpu.VMEM((width, hidden), BF),
             pltpu.VMEM((width, hidden), BF),
-            pltpu.VMEM((4, hidden, quarter), BF),
-            pltpu.SemaphoreType.DMA((6,)),
-            pltpu.SemaphoreType.DMA((4, RING)),
-            pltpu.SemaphoreType.DMA((4, RING)),
-            pltpu.SemaphoreType.DMA((4, RING)),
-            pltpu.SemaphoreType.DMA((4, RING)),
-            pltpu.SemaphoreType.DMA((RING,)),
-            pltpu.SemaphoreType.DMA((RING,)),
+            pltpu.VMEM((2, hidden, share), BF),
+            pltpu.SemaphoreType.DMA((4,)),
+            pltpu.SemaphoreType.DMA((4, HOPS + 1, chunks)),
+            pltpu.SemaphoreType.DMA((4, HOPS + 1, chunks)),
+            pltpu.SemaphoreType.DMA((4, HOPS, chunks)),
+            pltpu.SemaphoreType.DMA((4, HOPS, chunks)),
+            pltpu.SemaphoreType.DMA((2, HOPS)),
+            pltpu.SemaphoreType.DMA((2, HOPS)),
         ],
         compiler_params=pltpu.CompilerParams(
             collective_id=2, has_side_effects=True, vmem_limit_bytes=62 << 20
@@ -445,7 +504,7 @@
     both = jnp.stack([tokens, out_grad])
     send = jnp.einsum("tec,ktd->kecd", select_bf, both, preferred_element_type=F32).astype(BF)
     got = dispatch(send, count)
-    own = got.reshape(2 * count * capacity, 4, width // 4).transpose(1, 0, 2)
+    own = got.reshape(2 * count * capacity, 2, width // 2).transpose(1, 0, 2)
     sums, dot_sums = run_experts(own, gate_weight, up_weight, down_weight)
     sums = sums.transpose(1, 0, 2).reshape(2 * count, capacity, width // 2)
 

time: 338 us -> 225 us (0.67)
  Pallas kernels: 327 us -> 214 us
    pallas_call x1, Pallas kernels: 257 us -> 177 us  [run_experts(): pl.pallas_call(experts_kernel, out_shape=(jax.ShapeDtypeStruct((2, rows,...]
    pallas_call x1, Pallas kernels: 54 us -> 20.1 us  [giveback(): pl.pallas_call(functools.partial(giveback_kernel, count), out_shape=jax.S...]
where the time goes in v2:
time: 225 us
  Pallas kernels  214 us (95%)
  local copies, waits for them, and re-layouts  6.17 us (3%)
  matrix products  2.74 us (1%)
    pallas_call x1, Pallas kernels, run_experts(): pl.pallas_call(experts_kernel, out_shape=(jax.ShapeDtypeStruct((2, rows,...  177 us
    pallas_call x1, Pallas kernels, giveback(): pl.pallas_call(functools.partial(giveback_kernel, count), out_shape=jax.S...  20.1 us
    pallas_call x1, Pallas kernels, dispatch(): pl.pallas_call(functools.partial(dispatch_kernel, count), out_shape=jax.S...  16.3 us

profile of v2, /device:TPU:1, one launch (start us, length us, event | category | flops | bytes accessed | tf_op | source)
XLA Modules:
  0.0 225.2 jit_solution(14192995148233869378)
XLA Ops:
  0.6 0.0 copy-start
  0.6 0.7 convert_element_type.65
  1.3 0.8 slice_bitcast_fusion.1
  2.1 0.1 copy.59
  2.2 0.2 reduce_window_sum.11
  2.4 0.1 copy.60
  2.4 1.3 convolution_convert_fusion
  3.7 0.5 copy.86
  4.3 16.3 %dispatch.1 = bf16[16,3,6144]{2,1,0:T(4,128)(2,1)S(1)} custom-call(bf16[2,8,3,6144]{3,2,1,0:T(4,128)(2,1)S(1)} %bitcast.37), custom_call_target="tpu_custom_call" | custom-call | tf_op jit(solution)/shard_map/dispatch/pallas_call | solution.py:98
  20.6 0.7 reshape.287
  21.3 0.9 copy.87
  22.2 177.3 %experts.1 = (bf16[2,48,1536]{2,1,0:T(8,128)(2,1)}, f32[8,128]{1,0:T(8,128)}) custom-call(bf16[2,48,3072]{2,1,0:T(8,128)(2,1)} %bitcast.38, bf16[1,6144,256]{2,1,0:T(8,128)(2,1)} %wg_hbm.1, bf16[1,6144,256]{2,1,0:T(8,128)(2,1)} %wu_hbm.1, bf16[1,256,6144]{2,1,0:T(8,128)(2,1)} %wd_hbm.1), custom_call_target="tpu_custom_call" | custom-call | tf_op jit(solution)/shard_map/experts/pallas_call | solution.py:455
  199.5 0.0 copy-start.1
  199.5 0.0 copy-start.2
  199.5 1.3 copy.65
  200.8 0.7 slice_reduce_fusion
  201.5 0.1 reshape_squeeze.3
  201.6 0.2 copy.68
  201.8 0.2 copy.67
  202.1 0.1 fusion.12
  202.2 0.2 reshape.288
  202.4 0.2 pad_maximum_fusion.send_ref
  202.6 20.1 %giveback.1 = bf16[2,8,3,3200]{3,2,1,0:T(4,128)(2,1)S(1)} custom-call(bf16[16,3,3200]{2,1,0:T(4,128)(2,1)S(1)} %pad_maximum_fusion.send_ref), custom_call_target="tpu_custom_call" | custom-call | tf_op jit(solution)/shard_map/giveback/pallas_call | solution.py:168
  222.7 0.1 slice.33
  222.8 0.1 copy.71
  223.0 0.1 copy.72
  223.0 0.2 select_reduce_fusion.4
  223.2 0.0 copy-done.2
  223.3 0.6 pad_maximum_fusion.1
  223.8 0.1 copy.61
  223.9 0.3 fusion.2
  224.3 0.9 fusion.1
  (14 shorter events, 0.1 us)
Async XLA Ops:
  0.6 222.4 %copy-start = (bf16[6144,8]{0,1:T(8,128)(2,1)S(1)}, bf16[6144,8]{0,1:T(8,128)(2,1)}, u32[]{:S(2)}) copy-start(bf16[6144,8]{0,1:T(8,128)(2,1)} %param.12) | copy-start | bytes 294916
  199.5 23.6 %copy-start.1 = (bf16[8,6144]{1,0:T(8,128)(2,1)S(1)}, bf16[8,6144]{1,0:T(8,128)(2,1)}, u32[]{:S(2)}) copy-start(bf16[8,6144]{1,0:T(8,128)(2,1)} %param.8) | copy-start | bytes 294916
  199.5 23.7 %copy-start.2 = (s32[8]{0:T(128)S(1)}, s32[8]{0:T(128)}, u32[]{:S(2)}) copy-start(s32[8]{0:T(128)} %param.10) | copy-start | bytes 100

commit v3 on v2

v3 whole, which is shorter than its diff:
```python
import functools

import jax
import jax.numpy as jnp
from jax import lax
from jax.experimental import pallas as pl
from jax.experimental.pallas import tpu as pltpu
from jax.sharding import PartitionSpec as P

MESH = pl.DeviceIdType.MESH
BF = jnp.bfloat16
F32 = jnp.float32
RING = 32
HOPS = 16
GROUP = 4


def div(a, b):
    return a // b if isinstance(a, int) else lax.div(a, jnp.int32(b))


def rem(a, b):
    return a % b if isinstance(a, int) else lax.rem(a, jnp.int32(b))


def place(cycle, z, x):
    if cycle == 0:
        return 4 * z + rem(x + z, 4)
    turn = rem(z + 5 * x, 8)
    return 4 * x + 16 * div(turn, 4) + rem(turn, 4)


def coords(cycle, q):
    a, b = div(q, 4), rem(q, 4)
    if cycle == 0:
        return a, rem(b - a + 8, 4)
    return rem(3 * a + b, 8), rem(a, 4)


def peer(z, x):
    return {"seq": z, "mp": x}


def dot_nt(a, b, **kwargs):
    return lax.dot_general(a, b, (((1,), (1,)), ((), ())), preferred_element_type=F32, **kwargs)


def experts_kernel(
    send_ref, wg_hbm, wu_hbm, wd_hbm, back_ref, back_dots,
    got, flat, leave, xs, running, local, acc_t, acc_g, grads, dots, dot_slots, dot_out, wg, wu, wd,
    w_sem, in_own, in_send, in_recv, ag_send, ag_recv, rs_send, rs_recv, dot_send, dot_recv,
    out_own, out_send, out_recv,
):
    count = send_ref.shape[1]
    rows, share = xs.shape[2], xs.shape[3]
    hidden = wg.shape[1]
    part = share // 2
    half = 2 * part
    z, e, x = lax.axis_index("seq"), lax.axis_index("expert"), lax.axis_index("mp")
    other = x + 1 - 2 * rem(x, 2)
    own_kind = rem(x + z, 2)
    spot = [place(c, z, x) for c in range(2)]
    after = [coords(c, rem(spot[c] + 1, RING)) for c in range(2)]
    before = [coords(c, rem(spot[c] + RING - 1, RING)) for c in range(2)]
    to = [peer(*after[0]), peer(*before[0]), peer(*after[1]), peer(*before[1])]

    mates = [(j, mine) for j in range(count) for mine in (True, False) if j or not mine]

    def mate(j, mine):
        return {"seq": z, "expert": rem(e + j, count), "mp": x if mine else other}

    def column_slot(j, mine):
        return rem(x if mine else other, 2) * count + rem(e + j, count)

    loads = [
        pltpu.make_async_copy(wg_hbm.at[0], wg, w_sem.at[0]),
        pltpu.make_async_copy(wu_hbm.at[0], wu, w_sem.at[1]),
    ]
    for c in range(2):
        loads.append(pltpu.make_async_copy(wd_hbm.at[0, :, pl.ds(c * share, share)], wd.at[c], w_sem.at[2 + c]))

    barrier = pltpu.get_barrier_semaphore()
    for j, mine in mates:
        pl.semaphore_signal(barrier, inc=1, device_id=mate(j, mine), device_id_type=MESH)
    for r in range(4):
        pl.semaphore_signal(barrier, inc=1, device_id=to[r], device_id_type=MESH)
    pl.semaphore_wait(barrier, len(mates) + 4)

    my_slot = column_slot(0, True)
    own_copies = [
        pltpu.make_async_copy(send_ref.at[own_kind, e, k], got.at[k, my_slot], in_own.at[k]) for k in range(2)
    ]

    def bring(k, j, mine):
        return pltpu.make_async_remote_copy(
            src_ref=send_ref.at[own_kind if mine else 1 - own_kind, rem(e + j, count), k],
            dst_ref=got.at[k, my_slot],
            send_sem=in_send.at[k, 2 * j + (0 if mine else 1)], recv_sem=in_recv.at[k, my_slot],
            device_id=mate(j, mine), device_id_type=MESH,
        )

    def brought(k, j, mine):
        slot = column_slot(j, mine)
        return pltpu.make_async_remote_copy(
            src_ref=got.at[k, slot], dst_ref=got.at[k, slot],
            send_sem=in_send.at[k, 2 * j + (0 if mine else 1)], recv_sem=in_recv.at[k, slot],
            device_id=mate(j, mine), device_id_type=MESH,
        )

    for k in range(2):
        own_copies[k].start()
        for j, mine in mates:
            bring(k, j, mine).start()
    for load in loads:
        load.start()

    def held(r, s):
        c = r // 2
        return rem(spot[c] + RING - s, RING) if r % 2 == 0 else rem(spot[c] + s, RING)

    def gather(r, s, k, where):
        block = xs.at[r // 2, where, :, pl.ds(k * part, part)]
        return pltpu.make_async_remote_copy(
            src_ref=block, dst_ref=block, send_sem=ag_send.at[r, s, k], recv_sem=ag_recv.at[r, s, k],
            device_id=to[r], device_id_type=MESH,
        )

    tiles = part // 128
    for k in range(2):
        own_copies[k].wait()
        for j, mine in mates:
            brought(k, j, mine).wait_recv()
        length = got.shape[2]
        for i in range(2 * count):
            flat[i * length:(i + 1) * length, :] = got[k, i].astype(F32)
        for c in range(2):
            for j in range(tiles):
                block = flat[pl.ds(c * tiles + j, rows, stride=2 * tiles), :]
                begin = k * part + j * 128
                xs[c, spot[c], :, begin:begin + 128] = block.astype(BF)
        for r in range(4):
            gather(r, 1, k, spot[r // 2]).start()
    for load in loads:
        load.wait()

    def forward_unit(unit):
        b = div(unit, 4)
        c = div(rem(unit, 4), 2)
        kind = rem(unit, 2)
        p = spot[0] * (1 - c) + spot[1] * c
        begin = pl.multiple_of(c * share, share)

        def positions(parity):
            low = p - GROUP * (b + 1)
            low = low + rem(low + parity + 2 * RING, 2) + RING
            high = p + GROUP * b
            high = high + rem(high + parity, 2)
            return [div(rem(q, RING), 2) for q in (low, low + 2, high, high + 2)]

        @pl.when(kind == 0)
        def _():
            where = positions(0)
            lhs = jnp.concatenate([xs[c, 2 * t] for t in where], axis=0)
            gate = jnp.dot(lhs, wg[pl.ds(begin, share), :], preferred_element_type=F32)
            up = jnp.dot(lhs, wu[pl.ds(begin, share), :], preferred_element_type=F32)
            for i, t in enumerate(where):
                acc_t[c, t, :, :hidden] = gate[i * rows:(i + 1) * rows]
                acc_t[c, t, :, hidden:] = up[i * rows:(i + 1) * rows]

        @pl.when(kind == 1)
        def _():
            where = positions(1)
            lhs = jnp.concatenate([xs[c, 2 * t + 1] for t in where], axis=0)
            grad = dot_nt(lhs, wd[c])
            for i, t in enumerate(where):
                acc_g[c, t] = grad[i * rows:(i + 1) * rows]

    def ag_step(s, carry):
        for k in range(2):
            for r in range(4):
                gather(r, s, k, held(r, s)).wait_recv()
                if r % 2 == k:
                    gather(r, s + 1, k, held(r, s)).start()
                else:
                    @pl.when(s < HOPS - 1)
                    def _():
                        gather(r, s + 1, k, held(r, s)).start()

        @pl.when(s >= GROUP)
        def _():
            forward_unit(s - GROUP)

        return carry

    lax.fori_loop(1, HOPS, ag_step, 0)
    for r in range(4):
        gather(r, HOPS, r % 2, held(r, HOPS)).wait_recv()

    def tail_unit(u, carry):
        forward_unit(u)
        return carry

    lax.fori_loop(HOPS - GROUP, HOPS, tail_unit, 0)

    ones = jnp.ones((8, 128), F32)
    for pair in range(16):
        pz, px = pair // 2, 2 * (pair % 2)
        holders = [(pz, px), (pz, px + 1)]
        if (px + pz) % 2:
            holders = holders[::-1]
        t = [place(c, *holders[0]) // 2 for c in range(2)]
        g = [place(c, *holders[1]) // 2 for c in range(2)]
        pre_gate = acc_t[0, t[0], :, :hidden] + acc_t[1, t[1], :, :hidden]
        pre_up = acc_t[0, t[0], :, hidden:] + acc_t[1, t[1], :, hidden:]
        grad_hidden = acc_g[0, g[0]] + acc_g[1, g[1]]
        sigma = jax.nn.sigmoid(pre_gate)
        act = pre_gate * sigma
        inner = grad_hidden * act * pre_up
        grad_gate = (grad_hidden * pre_up * sigma * (1.0 + pre_gate * (1.0 - sigma))).astype(BF)
        grad_up = (grad_hidden * act).astype(BF)
        for c in range(2):
            for q in (2 * t[c], 2 * g[c] + 1):
                grads[c, q, :, :hidden] = grad_gate
                grads[c, q, :, hidden:] = grad_up
        folded = inner[:, 0:128]
        for i in range(1, hidden // 128):
            folded = folded + inner[:, i * 128:(i + 1) * 128]
        sums = dot_nt(ones, folded, precision=lax.Precision.HIGHEST)
        for q in (2 * t[0], 2 * g[0] + 1):
            dots[q, :, :rows] = sums

    def dest(r, s):
        c = r // 2
        return rem(spot[c] + HOPS + RING - s, RING) if r % 2 == 0 else rem(spot[c] + HOPS + s, RING)

    def backward_unit(unit):
        b = div(unit, 4)
        c = div(rem(unit, 4), 2)
        kind = rem(unit, 2)
        p = spot[0] * (1 - c) + spot[1] * c
        low = p + HOPS + RING - GROUP * b - (GROUP - 1)
        low = low + rem(low + kind, 2)
        high = p + HOPS + GROUP * b + 1
        high = high + rem(high + kind, 2)
        where = [2 * div(rem(q, RING), 2) + kind for q in (low, low + 2, high, high + 2)]
        lhs = jnp.concatenate([grads[c, q] for q in where], axis=0)
        begin = pl.multiple_of(kind * half + c * part, part)
        y = dot_nt(lhs[:, :hidden], wg[pl.ds(begin, part), :]) + dot_nt(lhs[:, hidden:], wu[pl.ds(begin, part), :])
        for i in range(GROUP):
            local[c, where[i]] = y[i * rows:(i + 1) * rows].astype(local.dtype)

    def head_unit(u, carry):
        backward_unit(u)
        return carry

    lax.fori_loop(0, GROUP, head_unit, 0)

    def scatter(r, s, k, src=None):
        lanes = pl.ds(k * (part // 2), part // 2)
        return pltpu.make_async_remote_copy(
            src_ref=running.at[r, s - 1, :, lanes] if src is None else src, dst_ref=running.at[r, s, :, lanes],
            send_sem=rs_send.at[r, s, k], recv_sem=rs_recv.at[r, s, k],
            device_id=to[r], device_id_type=MESH,
        )

    def scatter_local(r, s, k):
        return scatter(r, s, k, local.at[r // 2, dest(r, s), :, pl.ds(k * (part // 2), part // 2)])

    def add_local(r, s, k):
        lanes = slice(k * (part // 2), (k + 1) * (part // 2))
        total = running[r, s - 1, :, lanes].astype(F32) + local[r // 2, dest(r, s), :, lanes].astype(F32)
        running[r, s - 1, :, lanes] = total.astype(BF)

    def dot_copy(d, s, src):
        return pltpu.make_async_remote_copy(
            src_ref=src, dst_ref=dot_slots.at[d, s], send_sem=dot_send.at[d, s], recv_sem=dot_recv.at[d, s],
            device_id=to[d], device_id_type=MESH,
        )

    for r in range(4):
        scatter_local(r, 0, r % 2).start()
    for r in range(4):
        scatter_local(r, 1, 1 - r % 2).start()
    dot_copy(0, 0, dots.at[dest(0, 0)]).start()
    dot_copy(1, 1, dots.at[dest(1, 1)]).start()
    backward_unit(jnp.int32(GROUP))

    for r in range(4):
        scatter_local(r, 0, r % 2).wait_recv()
        add_local(r, 1, r % 2)
        scatter(r, 1, r % 2).start()
    dot_copy(0, 0, dot_slots.at[0, 0]).wait_recv()
    dot_slots[0, 0] = dot_slots[0, 0] + dots[dest(0, 1)]
    dot_copy(0, 1, dot_slots.at[0, 0]).start()
    backward_unit(jnp.int32(GROUP + 1))

    def rs_step(s, carry):
        for turn in range(2):
            for r in range(4):
                k = (r + 1 + turn) % 2
                scatter(r, s - 1, k).wait_recv()
                add_local(r, s, k)
                scatter(r, s, k).start()
        for d in range(2):
            dot_copy(d, s - 1, dot_slots.at[d, s - 1]).wait_recv()
            dot_slots[d, s - 1] = dot_slots[d, s - 1] + dots[dest(d, s)]
            dot_copy(d, s, dot_slots.at[d, s - 1]).start()

        @pl.when(s < HOPS - GROUP)
        def _():
            backward_unit(s + GROUP)

        return carry

    lax.fori_loop(2, HOPS, rs_step, 0)
    last = HOPS - 1
    tiles = part // 128
    for c in range(2):
        for k in range(2):
            for d in range(2):
                scatter(2 * c + d, last, k).wait_recv()
            lanes = slice(k * (part // 2), (k + 1) * (part // 2))
            total = running[2 * c, last, :, lanes].astype(F32) + running[2 * c + 1, last, :, lanes].astype(F32)
            total = total + local[c, spot[c], :, lanes].astype(F32)
            for j in range(tiles // 2):
                row = c * tiles + k * (tiles // 2) + j
                flat[pl.ds(row, rows, stride=2 * tiles), :] = total[:, j * 128:(j + 1) * 128]
    length = leave.shape[1]
    for i in range(2 * count):
        leave[i] = flat[i * length:(i + 1) * length, :].astype(BF)
    for d in range(2):
        dot_copy(d, last, dot_slots.at[d, last]).wait_recv()
    dot_out[...] = dot_slots[0, last] + dot_slots[1, last] + dots[spot[0]]

    def giveback(i, j, mine, src, dst):
        return pltpu.make_async_remote_copy(
            src_ref=src, dst_ref=dst,
            send_sem=out_send.at[i, 2 * j + (0 if mine else 1)], recv_sem=out_recv.at[i, own_kind * count + e],
            device_id=mate(j, mine), device_id_type=MESH,
        )

    def returned(i, j, mine, ref):
        kind, source = own_kind if mine else 1 - own_kind, rem(e + j, count)
        return pltpu.make_async_remote_copy(
            src_ref=ref.at[kind, source], dst_ref=ref.at[kind, source],
            send_sem=out_send.at[i, 2 * j + (0 if mine else 1)], recv_sem=out_recv.at[i, kind * count + source],
            device_id=mate(j, mine), device_id_type=MESH,
        )

    finals = [
        pltpu.make_async_copy(leave.at[my_slot], back_ref.at[own_kind, e], out_own.at[0]),
        pltpu.make_async_copy(dot_out, back_dots.at[own_kind, e], out_own.at[1]),
    ]
    for final in finals:
        final.start()
    sent = []
    for j, mine in mates:
        sent.append(giveback(0, j, mine, leave.at[column_slot(j, mine)], back_ref.at[own_kind, e]))
        sent.append(giveback(1, j, mine, dot_out, back_dots.at[own_kind, e]))
        sent[-2].start()
        sent[-1].start()

    for k in range(2):
        for j, mine in mates:
            bring(k, j, mine).wait_send()
    for r in range(4):
        gather(r, HOPS, r % 2, held(r, HOPS - 1)).wait_send()
        scatter_local(r, 0, r % 2).wait_send()
    dot_copy(0, 0, dots.at[dest(0, 0)]).wait_send()

    def drain(s, carry):
        for k in range(2):
            for r in range(4):
                gather(r, s, k, held(r, s - 1)).wait_send()
                scatter(r, s, k).wait_send()
        for d in range(2):
            dot_copy(d, s, dot_slots.at[d, s - 1]).wait_send()
        return carry

    lax.fori_loop(1, HOPS, drain, 0)
    for copy in sent:
        copy.wait_send()
    for final in finals:
        final.wait()
    for j, mine in mates:
        returned(0, j, mine, back_ref).wait_recv()
        returned(1, j, mine, back_dots).wait_recv()


def run_experts(send, gate_weight, up_weight, down_weight):
    count, length = send.shape[1], send.shape[3]
    width, hidden = gate_weight.shape[1:]
    share, part = width // 2, width // 4
    rows = 2 * count * length * 128 // (2 * part)
    vmem = pl.BlockSpec(memory_space=pltpu.VMEM)
    hbm = pl.BlockSpec(memory_space=pl.ANY)
    return pl.pallas_call(
        experts_kernel,
        out_shape=(
            jax.ShapeDtypeStruct((2, count, length, 128), BF),
            jax.ShapeDtypeStruct((2, count, 8, 128), F32),
        ),
        in_specs=[vmem, hbm, hbm, hbm],
        out_specs=(vmem, vmem),
        scratch_shapes=[
            pltpu.VMEM((2, 2 * count, length, 128), BF),
            pltpu.VMEM((2 * count * length, 128), F32),
            pltpu.VMEM((2 * count, length, 128), BF),
            pltpu.VMEM((2, RING, rows, share), BF),
            pltpu.VMEM((4, HOPS, rows, part), BF),
            pltpu.VMEM((2, RING, rows, part), BF),
            pltpu.VMEM((2, 16, rows, 2 * hidden), F32),
            pltpu.VMEM((2, 16, rows, hidden), F32),
            pltpu.VMEM((2, RING, rows, 2 * hidden), BF),
            pltpu.VMEM((RING, 8, 128), F32),
            pltpu.VMEM((2, HOPS, 8, 128), F32),
            pltpu.VMEM((8, 128), F32),
            pltpu.VMEM((width, hidden), BF),
            pltpu.VMEM((width, hidden), BF),
            pltpu.VMEM((2, hidden, share), BF),
            pltpu.SemaphoreType.DMA((4,)),
            pltpu.SemaphoreType.DMA((2,)),
            pltpu.SemaphoreType.DMA((2, 2 * count)),
            pltpu.SemaphoreType.DMA((2, 2 * count)),
            pltpu.SemaphoreType.DMA((4, HOPS + 1, 2)),
            pltpu.SemaphoreType.DMA((4, HOPS + 1, 2)),
            pltpu.SemaphoreType.DMA((4, HOPS, 2)),
            pltpu.SemaphoreType.DMA((4, HOPS, 2)),
            pltpu.SemaphoreType.DMA((2, HOPS)),
            pltpu.SemaphoreType.DMA((2, HOPS)),
            pltpu.SemaphoreType.DMA((2,)),
            pltpu.SemaphoreType.DMA((2, 2 * count)),
            pltpu.SemaphoreType.DMA((2, 2 * count)),
        ],
        compiler_params=pltpu.CompilerParams(
            collective_id=0, has_side_effects=True, vmem_limit_bytes=63 << 20
        ),
        name="experts",
    )(send, gate_weight, up_weight, down_weight)


def on_device(tokens, out_grad, kept_mask, routes, router, gate_weight, up_weight, down_weight):
    row_count, width = tokens.shape
    count = lax.axis_size("expert")
    capacity = 3 * row_count // 8
    columns = lax.broadcasted_iota(jnp.int32, (row_count, count), 1)
    first_hot = (routes[:, 0:1] == columns).astype(F32)
    second_hot = (routes[:, 1:2] == columns).astype(F32)
    keep_rows = kept_mask.astype(F32)
    chosen = ((first_hot + second_hot) * keep_rows[:, None]).astype(jnp.int32)
    position = jnp.cumsum(chosen, axis=0) - 1
    slot_iota = lax.broadcasted_iota(jnp.int32, (row_count, count, capacity), 2)
    select_mask = (chosen[:, :, None] == 1) & (position[:, :, None] == slot_iota)
    select_bf = select_mask.astype(BF)
    select_full = select_mask.astype(F32)
    both = jnp.stack([tokens, out_grad])
    send = jnp.einsum("tec,ktd->kecd", select_bf, both, preferred_element_type=F32).astype(BF)
    tiles = width // 512
    send = send.reshape(2, count, capacity, 2, 2, tiles, 128).transpose(0, 1, 4, 2, 3, 5, 6)
    send = send.reshape(2, count, 2, capacity * 2 * tiles, 128)
    back, back_dots = run_experts(send, gate_weight, up_weight, down_weight)
    back = back.reshape(2, count, capacity, width // 2)
    own_slot = rem(lax.axis_index("mp"), 2) * count + lax.axis_index("expert")
    dot_back = lax.dynamic_slice_in_dim(back_dots[0, :, 0, :], own_slot * capacity, capacity, 1)

    logits = jnp.dot(tokens, router, preferred_element_type=F32)
    first_logit = jnp.sum(logits * first_hot, axis=1)
    second_logit = jnp.sum(logits * second_hot, axis=1)
    gate_first = jax.nn.sigmoid(first_logit - second_logit)
    gate_second = jax.nn.sigmoid(second_logit - first_logit)
    gate_table = (first_hot * gate_first[:, None] + second_hot * gate_second[:, None]).astype(BF)
    weigh = select_bf * gate_table[:, :, None]
    expert_sum = jnp.einsum("tec,kecd->tkd", weigh, back, preferred_element_type=F32)
    expert_sum = expert_sum.reshape(row_count, width)
    dot_table = jnp.sum(select_full * dot_back[None], axis=2)
    dot_first = jnp.sum(dot_table * first_hot, axis=1)
    dot_second = jnp.sum(dot_table * second_hot, axis=1)
    product = gate_first * gate_second * keep_rows
    grad_first = product * (dot_first - dot_second)
    grad_second = product * (dot_second - dot_first)
    logit_grad = first_hot * grad_first[:, None] + second_hot * grad_second[:, None]
    router_term = jnp.dot(logit_grad, router.astype(F32).T, precision=lax.Precision.HIGHEST)
    d_tokens = ((expert_sum + router_term) * keep_rows[:, None]).astype(BF)
    gate_grad = jnp.stack([grad_first, grad_second], axis=1)
    return (d_tokens, gate_grad)


def solution(mesh):
    return jax.shard_map(
        on_device,
        mesh=mesh,
        in_specs=(
            P(("seq", "expert", "mp"), None),
            P(("seq", "expert", "mp"), None),
            P(("seq", "expert", "mp")),
            P(("seq", "expert", "mp"), None),
            P(),
            P("expert", None, ("seq", "mp")),
            P("expert", None, ("seq", "mp")),
            P("expert", ("seq", "mp"), None),
        ),
        out_specs=(P(("seq", "expert", "mp"), None), P(("seq", "expert", "mp"), None)),
        check_vma=False,
    )
```

time: 225 us -> 217 us (0.964)
  Pallas kernels: 214 us -> 208 us
    pallas_call x3 -> x1, Pallas kernels: 214 us -> 208 us  [run_experts(): pl.pallas_call(experts_kernel, out_shape=(jax.ShapeDtypeStruct((2, count,...]
where the time goes in v3:
time: 217 us
  Pallas kernels  208 us (96%)
  local copies, waits for them, and re-layouts  4.56 us (2%)
  matrix products  2.65 us (1%)
    pallas_call x1, Pallas kernels, run_experts(): pl.pallas_call(experts_kernel, out_shape=(jax.ShapeDtypeStruct((2, count,...  208 us

profile of v3, /device:TPU:1, one launch (start us, length us, event | category | flops | bytes accessed | tf_op | source)
XLA Modules:
  0.0 217.0 jit_solution(9257350893151996473)
XLA Ops:
  0.6 0.0 copy-start
  0.6 0.7 convert_element_type.57
  1.3 0.8 slice_bitcast_fusion.1
  2.1 0.2 reduce_window_sum.11
  2.3 0.1 copy.33
  2.4 0.1 copy.32
  2.4 1.3 convolution_convert_fusion
  3.7 0.1 copy.36
  3.8 0.9 copy.37.send_ref
  4.7 0.0 copy-start.1
  4.7 0.0 copy-start.2
  4.7 207.5 %experts.1 = (bf16[2,8,72,128]{3,2,1,0:T(8,128)(2,1)}, f32[2,8,8,128]{3,2,1,0:T(8,128)}) custom-call(bf16[2,8,2,72,128]{4,3,2,1,0:T(8,128)(2,1)} %copy.37.send_ref, bf16[1,6144,256]{2,1,0:T(8,128)(2,1)} %wg_hbm.1, bf16[1,6144,256]{2,1,0:T(8,128)(2,1)} %wu_hbm.1, bf16[1,256,6144]{2,1,0:T(8,128)(2,1)} %wd_hbm.1), custom_call_target="tpu_custom_call" | custom-call | tf_op jit(solution)/shard_map/experts/pallas_call | solution.py:397
  212.3 1.0 reshape.228
  213.3 0.4 copy.38
  213.7 0.2 dot_general.19
  213.9 0.8 slice.17
  214.6 0.1 constant_dynamic-slice_fusion
  214.7 0.1 copy.39
  214.8 0.1 copy.40
  214.9 0.0 copy-done
  214.9 0.0 copy-done.1
  214.9 0.2 select_reduce_fusion.4
  215.1 0.0 copy-done.2
  215.1 0.1 copy.34
  215.2 0.2 convolution_bitcast_fusion
  215.5 0.9 fusion.1
  216.4 0.6 pad_maximum_fusion
  (7 shorter events, 0.1 us)
Async XLA Ops:
  0.6 214.3 %copy-start = (bf16[6144,8]{0,1:T(8,128)(2,1)S(1)}, bf16[6144,8]{0,1:T(8,128)(2,1)}, u32[]{:S(2)}) copy-start(bf16[6144,8]{0,1:T(8,128)(2,1)} %param.12) | copy-start | bytes 294916
  4.7 210.2 %copy-start.1 = (bf16[8,6144]{1,0:T(8,128)(2,1)S(1)}, bf16[8,6144]{1,0:T(8,128)(2,1)}, u32[]{:S(2)}) copy-start(bf16[8,6144]{1,0:T(8,128)(2,1)} %param.8) | copy-start | bytes 294916
  4.7 210.4 %copy-start.2 = (s32[8]{0:T(128)S(1)}, s32[8]{0:T(128)}, u32[]{:S(2)}) copy-start(s32[8]{0:T(128)} %param.10) | copy-start | bytes 100

commit v4 on v3

--- a/solution.py
+++ b/solution.py
@@ -13,6 +13,7 @@
 RING = 32
 HOPS = 16
 GROUP = 4
+CUTS = 4
 
 
 def div(a, b):
@@ -46,12 +47,13 @@
 
 
 def experts_kernel(
-    send_ref, wg_hbm, wu_hbm, wd_hbm, back_ref, back_dots,
-    got, flat, leave, xs, running, local, acc_t, acc_g, grads, dots, dot_slots, dot_out, wg, wu, wd,
+    plan_ref, tok_ref, grad_ref, wg_hbm, wu_hbm, wd_hbm, back_ref, back_dots,
+    send_ref, got, flat, leave, xs, running, local, acc_t, acc_g, grads, dots, dot_slots, dot_out, wg, wu, wd,
     w_sem, in_own, in_send, in_recv, ag_send, ag_recv, rs_send, rs_recv, dot_send, dot_recv,
     out_own, out_send, out_recv,
 ):
-    count = send_ref.shape[1]
+    count = send_ref.shape[2]
+    capacity = 3 * tok_ref.shape[0] // 8
     rows, share = xs.shape[2], xs.shape[3]
     hidden = wg.shape[1]
     part = share // 2
@@ -84,16 +86,42 @@
         pl.semaphore_signal(barrier, inc=1, device_id=mate(j, mine), device_id_type=MESH)
     for r in range(4):
         pl.semaphore_signal(barrier, inc=1, device_id=to[r], device_id_type=MESH)
+    tiles = part // 128
+    row = lax.broadcasted_iota(jnp.int32, (count * capacity, 128), 0)
+    expert = jnp.zeros((count * capacity, 128), jnp.int32)
+    for m in range(1, count):
+        expert = expert + (row >= m * capacity).astype(jnp.int32)
+    place_in = (row - capacity * expert + 1).astype(F32)
+    expert = expert.astype(F32)
+    named = (plan_ref[0:1, :] == expert) | (plan_ref[1:2, :] == expert)
+    chosen = jnp.where(named, plan_ref[2:3, :], 0.0)
+    upto = lax.broadcasted_iota(jnp.int32, (128, 128), 0) <= lax.broadcasted_iota(jnp.int32, (128, 128), 1)
+    nth = jnp.dot(chosen.astype(BF), upto.astype(F32).astype(BF), preferred_element_type=F32)
+    pick = jnp.where(nth == place_in, chosen, 0.0).astype(BF)[:, : tok_ref.shape[0]]
+    length = send_ref.shape[3]
+    for kind, source in enumerate((tok_ref, grad_ref)):
+        for c in range(2):
+            for k in range(2):
+                begin = c * share + k * part
+                picked = jnp.dot(pick, source[:, begin:begin + part], preferred_element_type=F32)
+                for j in range(tiles):
+                    where = k * count * length + c * tiles + j
+                    flat[pl.ds(where, count * capacity, stride=2 * tiles), :] = picked[:, j * 128:(j + 1) * 128]
+        for k in range(2):
+            for i in range(count):
+                begin = (k * count + i) * length
+                send_ref[kind, k, i] = flat[begin:begin + length, :].astype(BF)
+
     pl.semaphore_wait(barrier, len(mates) + 4)
 
     my_slot = column_slot(0, True)
     own_copies = [
-        pltpu.make_async_copy(send_ref.at[own_kind, e, k], got.at[k, my_slot], in_own.at[k]) for k in range(2)
+        pltpu.make_async_copy(send_ref.at[own_kind, k, e], got.at[k, my_slot], in_own.at[k]) for k in range(2)
     ]
 
     def bring(k, j, mine):
         return pltpu.make_async_remote_copy(
-            src_ref=send_ref.at[own_kind if mine else 1 - own_kind, rem(e + j, count), k],
+            src_ref=send_ref.at[own_kind if mine else 1 - own_kind, k, rem(e + j, count)],
             dst_ref=got.at[k, my_slot],
             send_sem=in_send.at[k, 2 * j + (0 if mine else 1)], recv_sem=in_recv.at[k, my_slot],
             device_id=mate(j, mine), device_id_type=MESH,
@@ -125,7 +153,6 @@
             device_id=to[r], device_id_type=MESH,
         )
 
-    tiles = part // 128
     for k in range(2):
         own_copies[k].wait()
         for j, mine in mates:
@@ -249,55 +276,62 @@
         for i in range(GROUP):
             local[c, where[i]] = y[i * rows:(i + 1) * rows].astype(local.dtype)
 
+    cut = part // CUTS
+    mine_of = [[d * (CUTS // 2) + i for i in range(CUTS // 2)] for d in range(2)]
+
+    def scatter(r, s, k, src=None):
+        lanes = pl.ds(k * cut, cut)
+        return pltpu.make_async_remote_copy(
+            src_ref=running.at[r, s - 1, :, lanes] if src is None else src, dst_ref=running.at[r, s, :, lanes],
+            send_sem=rs_send.at[r, s, k], recv_sem=rs_recv.at[r, s, k],
+            device_id=to[r], device_id_type=MESH,
+        )
+
+    def scatter_local(r, s, k):
+        return scatter(r, s, k, local.at[r // 2, dest(r, s), :, pl.ds(k * cut, cut)])
+
+    def add_local(r, s, k):
+        lanes = slice(k * cut, (k + 1) * cut)
+        total = running[r, s - 1, :, lanes].astype(F32) + local[r // 2, dest(r, s), :, lanes].astype(F32)
+        running[r, s - 1, :, lanes] = total.astype(BF)
+
+    def dot_copy(d, s, src):
+        return pltpu.make_async_remote_copy(
+            src_ref=src, dst_ref=dot_slots.at[d, s], send_sem=dot_send.at[d, s], recv_sem=dot_recv.at[d, s],
+            device_id=to[d], device_id_type=MESH,
+        )
+
     def head_unit(u, carry):
         backward_unit(u)
         return carry
 
-    lax.fori_loop(0, GROUP, head_unit, 0)
-
-    def scatter(r, s, k, src=None):
-        lanes = pl.ds(k * (part // 2), part // 2)
-        return pltpu.make_async_remote_copy(
-            src_ref=running.at[r, s - 1, :, lanes] if src is None else src, dst_ref=running.at[r, s, :, lanes],
-            send_sem=rs_send.at[r, s, k], recv_sem=rs_recv.at[r, s, k],
-            device_id=to[r], device_id_type=MESH,
-        )
-
-    def scatter_local(r, s, k):
-        return scatter(r, s, k, local.at[r // 2, dest(r, s), :, pl.ds(k * (part // 2), part // 2)])
-
-    def add_local(r, s, k):
-        lanes = slice(k * (part // 2), (k + 1) * (part // 2))
-        total = running[r, s - 1, :, lanes].astype(F32) + local[r // 2, dest(r, s), :, lanes].astype(F32)
-        running[r, s - 1, :, lanes] = total.astype(BF)
-
-    def dot_copy(d, s, src):
-        return pltpu.make_async_remote_copy(
-            src_ref=src, dst_ref=dot_slots.at[d, s], send_sem=dot_send.at[d, s], recv_sem=dot_recv.at[d, s],
-            device_id=to[d], device_id_type=MESH,
-        )
-
-    for r in range(4):
-        scatter_local(r, 0, r % 2).start()
-    for r in range(4):
-        scatter_local(r, 1, 1 - r % 2).start()
+    for c in range(2):
+        lax.fori_loop(2 * c, 2 * c + 2, head_unit, 0)
+        for r in (2 * c, 2 * c + 1):
+            for k in mine_of[r % 2]:
+                scatter_local(r, 0, k).start()
+        for r in (2 * c, 2 * c + 1):
+            for k in mine_of[1 - r % 2]:
+                scatter_local(r, 1, k).start()
     dot_copy(0, 0, dots.at[dest(0, 0)]).start()
     dot_copy(1, 1, dots.at[dest(1, 1)]).start()
     backward_unit(jnp.int32(GROUP))
 
-    for r in range(4):
-        scatter_local(r, 0, r % 2).wait_recv()
-        add_local(r, 1, r % 2)
-        scatter(r, 1, r % 2).start()
+    for i in range(CUTS // 2):
+        for r in range(4):
+            k = mine_of[r % 2][i]
+            scatter_local(r, 0, k).wait_recv()
+            add_local(r, 1, k)
+            scatter(r, 1, k).start()
     dot_copy(0, 0, dot_slots.at[0, 0]).wait_recv()
     dot_slots[0, 0] = dot_slots[0, 0] + dots[dest(0, 1)]
     dot_copy(0, 1, dot_slots.at[0, 0]).start()
     backward_unit(jnp.int32(GROUP + 1))
 
     def rs_step(s, carry):
-        for turn in range(2):
+        for turn in range(CUTS):
             for r in range(4):
-                k = (r + 1 + turn) % 2
+                k = (mine_of[1 - r % 2] + mine_of[r % 2])[turn]
                 scatter(r, s - 1, k).wait_recv()
                 add_local(r, s, k)
                 scatter(r, s, k).start()
@@ -316,15 +350,15 @@
     last = HOPS - 1
     tiles = part // 128
     for c in range(2):
-        for k in range(2):
+        for k in range(CUTS):
             for d in range(2):
                 scatter(2 * c + d, last, k).wait_recv()
-            lanes = slice(k * (part // 2), (k + 1) * (part // 2))
+            lanes = slice(k * cut, (k + 1) * cut)
             total = running[2 * c, last, :, lanes].astype(F32) + running[2 * c + 1, last, :, lanes].astype(F32)
             total = total + local[c, spot[c], :, lanes].astype(F32)
-            for j in range(tiles // 2):
-                row = c * tiles + k * (tiles // 2) + j
-                flat[pl.ds(row, rows, stride=2 * tiles), :] = total[:, j * 128:(j + 1) * 128]
+            for j in range(tiles // CUTS):
+                line = c * tiles + k * (tiles // CUTS) + j
+                flat[pl.ds(line, rows, stride=2 * tiles), :] = total[:, j * 128:(j + 1) * 128]
     length = leave.shape[1]
     for i in range(2 * count):
         leave[i] = flat[i * length:(i + 1) * length, :].astype(BF)
@@ -365,13 +399,16 @@
             bring(k, j, mine).wait_send()
     for r in range(4):
         gather(r, HOPS, r % 2, held(r, HOPS - 1)).wait_send()
-        scatter_local(r, 0, r % 2).wait_send()
+        for k in mine_of[r % 2]:
+            scatter_local(r, 0, k).wait_send()
     dot_copy(0, 0, dots.at[dest(0, 0)]).wait_send()
 
     def drain(s, carry):
         for k in range(2):
             for r in range(4):
                 gather(r, s, k, held(r, s - 1)).wait_send()
+        for k in range(CUTS):
+            for r in range(4):
                 scatter(r, s, k).wait_send()
         for d in range(2):
             dot_copy(d, s, dot_slots.at[d, s - 1]).wait_send()
@@ -387,11 +424,12 @@
         returned(1, j, mine, back_dots).wait_recv()
 
 
-def run_experts(send, gate_weight, up_weight, down_weight):
-    count, length = send.shape[1], send.shape[3]
+def run_experts(count, plan, tokens, out_grad, gate_weight, up_weight, down_weight):
     width, hidden = gate_weight.shape[1:]
     share, part = width // 2, width // 4
-    rows = 2 * count * length * 128 // (2 * part)
+    capacity = 3 * tokens.shape[0] // 8
+    length = capacity * 2 * part // 128
+    rows = 2 * count * capacity
     vmem = pl.BlockSpec(memory_space=pltpu.VMEM)
     hbm = pl.BlockSpec(memory_space=pl.ANY)
     return pl.pallas_call(
@@ -400,9 +438,10 @@
             jax.ShapeDtypeStruct((2, count, length, 128), BF),
             jax.ShapeDtypeStruct((2, count, 8, 128), F32),
         ),
-        in_specs=[vmem, hbm, hbm, hbm],
+        in_specs=[vmem, vmem, vmem, hbm, hbm, hbm],
         out_specs=(vmem, vmem),
         scratch_shapes=[
+            pltpu.VMEM((2, 2, count, length, 128), BF),
             pltpu.VMEM((2, 2 * count, length, 128), BF),
             pltpu.VMEM((2 * count * length, 128), F32),
             pltpu.VMEM((2 * count, length, 128), BF),
@@ -424,8 +463,8 @@
             pltpu.SemaphoreType.DMA((2, 2 * count)),
             pltpu.SemaphoreType.DMA((4, HOPS + 1, 2)),
             pltpu.SemaphoreType.DMA((4, HOPS + 1, 2)),
-            pltpu.SemaphoreType.DMA((4, HOPS, 2)),
-            pltpu.SemaphoreType.DMA((4, HOPS, 2)),
+            pltpu.SemaphoreType.DMA((4, HOPS, CUTS)),
+            pltpu.SemaphoreType.DMA((4, HOPS, CUTS)),
             pltpu.SemaphoreType.DMA((2, HOPS)),
             pltpu.SemaphoreType.DMA((2, HOPS)),
             pltpu.SemaphoreType.DMA((2,)),
@@ -436,7 +475,7 @@
             collective_id=0, has_side_effects=True, vmem_limit_bytes=63 << 20
         ),
         name="experts",
-    )(send, gate_weight, up_weight, down_weight)
+    )(plan, tokens, out_grad, gate_weight, up_weight, down_weight)
 
 
 def on_device(tokens, out_grad, kept_mask, routes, router, gate_weight, up_weight, down_weight):
@@ -453,12 +492,9 @@
     select_mask = (chosen[:, :, None] == 1) & (position[:, :, None] == slot_iota)
     select_bf = select_mask.astype(BF)
     select_full = select_mask.astype(F32)
-    both = jnp.stack([tokens, out_grad])
-    send = jnp.einsum("tec,ktd->kecd", select_bf, both, preferred_element_type=F32).astype(BF)
-    tiles = width // 512
-    send = send.reshape(2, count, capacity, 2, 2, tiles, 128).transpose(0, 1, 4, 2, 3, 5, 6)
-    send = send.reshape(2, count, 2, capacity * 2 * tiles, 128)
-    back, back_dots = run_experts(send, gate_weight, up_weight, down_weight)
+    plan = jnp.concatenate([routes.astype(F32).T, keep_rows[None]], axis=0)
+    plan = jnp.pad(plan, ((0, 5), (0, 128 - row_count)))
+    back, back_dots = run_experts(count, plan, tokens, out_grad, gate_weight, up_weight, down_weight)
     back = back.reshape(2, count, capacity, width // 2)
     own_slot = rem(lax.axis_index("mp"), 2) * count + lax.axis_index("expert")
     dot_back = lax.dynamic_slice_in_dim(back_dots[0, :, 0, :], own_slot * capacity, capacity, 1)

time: 217 us -> 211 us (0.972)
  Pallas kernels: 208 us -> 202 us
    pallas_call x1, Pallas kernels: 208 us -> 202 us  [run_experts(): pl.pallas_call(experts_kernel, out_shape=(jax.ShapeDtypeStruct((2, count,...]
where the time goes in v4:
time: 211 us; the launch traced here: 210 us
  Pallas kernels  202 us (96%)
  local copies, waits for them, and re-layouts  3.62 us (2%)
  other arithmetic  2.77 us (1%)
    pallas_call x1, Pallas kernels, run_experts(): pl.pallas_call(experts_kernel, out_shape=(jax.ShapeDtypeStruct((2, count,...  202 us

profile of v4, /device:TPU:1, one launch (start us, length us, event | category | flops | bytes accessed | tf_op | source)
XLA Modules:
  0.0 210.5 jit_solution(7104232578835858402)
XLA Ops:
  0.6 0.0 copy-start
  0.7 0.7 convert_bitcast_fusion
  1.4 0.8 slice_bitcast_fusion.1
  2.1 0.7 fusion.19
  2.8 0.1 copy.24
  2.9 0.6 select_maximum_fusion.plan_ref
  3.5 0.2 reduce_window_sum.11
  3.7 0.1 copy.25
  3.7 0.0 copy-start.1
  3.7 0.0 copy-start.2
  3.7 202.0 %experts.1 = (bf16[2,8,72,128]{3,2,1,0:T(8,128)(2,1)}, f32[2,8,8,128]{3,2,1,0:T(8,128)}) custom-call(f32[8,128]{1,0:T(8,128)} %select_maximum_fusion.plan_ref, bf16[8,6144]{1,0:T(8,128)(2,1)} %tok_ref.1, bf16[8,6144]{1,0:T(8,128)(2,1)} %grad_ref.1, bf16[1,6144,256]{2,1,0:T(8,128)(2,1)} %wg_hbm.1, bf16[1,6144,256]{2,1,0:T(8,128)(2,1)} %wu_hbm.1, ...), custom_call_target="tpu_custom_call" | custom-call | tf_op jit(solution)/shard_map/experts/pallas_call | solution.py:435
  205.8 0.8 slice.17
  206.5 0.1 constant_dynamic-slice_fusion
  206.6 0.1 copy.28
  206.7 0.1 copy.29
  206.8 0.0 copy-done
  206.8 0.0 copy-done.1
  206.8 0.2 select_reduce_fusion.4
  207.0 0.0 copy-done.2
  207.0 0.6 pad_maximum_fusion
  207.6 0.1 copy.26
  207.7 1.0 reshape.220
  208.7 0.4 copy.27
  209.1 0.2 dot_general.15
  209.3 0.2 convolution_bitcast_fusion
  209.5 0.9 fusion.1
  (7 shorter events, 0.1 us)
Async XLA Ops:
  0.6 206.2 %copy-start = (bf16[6144,8]{0,1:T(8,128)(2,1)S(1)}, bf16[6144,8]{0,1:T(8,128)(2,1)}, u32[]{:S(2)}) copy-start(bf16[6144,8]{0,1:T(8,128)(2,1)} %param.12) | copy-start | bytes 294916
  3.7 203.1 %copy-start.1 = (bf16[8,6144]{1,0:T(8,128)(2,1)S(1)}, bf16[8,6144]{1,0:T(8,128)(2,1)}, u32[]{:S(2)}) copy-start(bf16[8,6144]{1,0:T(8,128)(2,1)} %tok_ref.1) | copy-start | bytes 294916
  3.7 203.2 %copy-start.2 = (s32[8]{0:T(128)S(1)}, s32[8]{0:T(128)}, u32[]{:S(2)}) copy-start(s32[8]{0:T(128)} %param.10) | copy-start | bytes 100

commit v5 on v4

--- a/solution.py
+++ b/solution.py
@@ -49,7 +49,7 @@
 def experts_kernel(
     plan_ref, tok_ref, grad_ref, wg_hbm, wu_hbm, wd_hbm, back_ref, back_dots,
     send_ref, got, flat, leave, xs, running, local, acc_t, acc_g, grads, dots, dot_slots, dot_out, wg, wu, wd,
-    w_sem, in_own, in_send, in_recv, ag_send, ag_recv, rs_send, rs_recv, dot_send, dot_recv,
+    w_sem, in_own, in_send, in_recv, ag_send, ag_recv, rs_first, rs_send, rs_recv, dot_send, dot_recv,
     out_own, out_send, out_recv,
 ):
     count = send_ref.shape[2]
@@ -123,17 +123,17 @@
         return pltpu.make_async_remote_copy(
             src_ref=send_ref.at[own_kind if mine else 1 - own_kind, k, rem(e + j, count)],
             dst_ref=got.at[k, my_slot],
-            send_sem=in_send.at[k, 2 * j + (0 if mine else 1)], recv_sem=in_recv.at[k, my_slot],
+            send_sem=in_send.at[k], recv_sem=in_recv.at[k],
             device_id=mate(j, mine), device_id_type=MESH,
         )
 
-    def brought(k, j, mine):
-        slot = column_slot(j, mine)
+    def bulk(ref, send_sem, recv_sem):
         return pltpu.make_async_remote_copy(
-            src_ref=got.at[k, slot], dst_ref=got.at[k, slot],
-            send_sem=in_send.at[k, 2 * j + (0 if mine else 1)], recv_sem=in_recv.at[k, slot],
-            device_id=mate(j, mine), device_id_type=MESH,
+            src_ref=ref, dst_ref=ref, send_sem=send_sem, recv_sem=recv_sem, device_id=to[0], device_id_type=MESH
         )
+
+    def brought(k):
+        return bulk(got.at[k, pl.ds(0, len(mates))], in_send.at[k], in_recv.at[k])
 
     for k in range(2):
         own_copies[k].start()
@@ -149,14 +149,13 @@
     def gather(r, s, k, where):
         block = xs.at[r // 2, where, :, pl.ds(k * part, part)]
         return pltpu.make_async_remote_copy(
-            src_ref=block, dst_ref=block, send_sem=ag_send.at[r, s, k], recv_sem=ag_recv.at[r, s, k],
+            src_ref=block, dst_ref=block, send_sem=ag_send.at[r], recv_sem=ag_recv.at[r % 2, s, k],
             device_id=to[r], device_id_type=MESH,
         )
 
     for k in range(2):
         own_copies[k].wait()
-        for j, mine in mates:
-            brought(k, j, mine).wait_recv()
+        brought(k).wait_recv()
         length = got.shape[2]
         for i in range(2 * count):
             flat[i * length:(i + 1) * length, :] = got[k, i].astype(F32)
@@ -202,16 +201,20 @@
             for i, t in enumerate(where):
                 acc_g[c, t] = grad[i * rows:(i + 1) * rows]
 
+    def gathered(d, s, k):
+        return bulk(local.at[0, pl.ds(0, 2)], ag_send.at[d], ag_recv.at[d, s, k])
+
     def ag_step(s, carry):
         for k in range(2):
-            for r in range(4):
-                gather(r, s, k, held(r, s)).wait_recv()
-                if r % 2 == k:
-                    gather(r, s + 1, k, held(r, s)).start()
-                else:
-                    @pl.when(s < HOPS - 1)
-                    def _():
+            for d in range(2):
+                gathered(d, s, k).wait_recv()
+                for r in (d, d + 2):
+                    if d == k:
                         gather(r, s + 1, k, held(r, s)).start()
+                    else:
+                        @pl.when(s < HOPS - 1)
+                        def _():
+                            gather(r, s + 1, k, held(r, s)).start()
 
         @pl.when(s >= GROUP)
         def _():
@@ -220,8 +223,8 @@
         return carry
 
     lax.fori_loop(1, HOPS, ag_step, 0)
-    for r in range(4):
-        gather(r, HOPS, r % 2, held(r, HOPS)).wait_recv()
+    for d in range(2):
+        gathered(d, HOPS, d).wait_recv()
 
     def tail_unit(u, carry):
         forward_unit(u)
@@ -279,16 +282,19 @@
     cut = part // CUTS
     mine_of = [[d * (CUTS // 2) + i for i in range(CUTS // 2)] for d in range(2)]
 
-    def scatter(r, s, k, src=None):
+    def scatter(r, s, k, src=None, first=False):
         lanes = pl.ds(k * cut, cut)
         return pltpu.make_async_remote_copy(
             src_ref=running.at[r, s - 1, :, lanes] if src is None else src, dst_ref=running.at[r, s, :, lanes],
-            send_sem=rs_send.at[r, s, k], recv_sem=rs_recv.at[r, s, k],
+            send_sem=(rs_first if first else rs_send).at[r], recv_sem=rs_recv.at[r % 2, s, k],
             device_id=to[r], device_id_type=MESH,
         )
 
     def scatter_local(r, s, k):
-        return scatter(r, s, k, local.at[r // 2, dest(r, s), :, pl.ds(k * cut, cut)])
+        return scatter(r, s, k, local.at[r // 2, dest(r, s), :, pl.ds(k * cut, cut)], s == 0)
+
+    def scattered(d, s, k):
+        return bulk(running.at[pl.ds(0, 2), 0, :, pl.ds(0, cut)], rs_send.at[d], rs_recv.at[d, s, k])
 
     def add_local(r, s, k):
         lanes = slice(k * cut, (k + 1) * cut)
@@ -297,9 +303,12 @@
 
     def dot_copy(d, s, src):
         return pltpu.make_async_remote_copy(
-            src_ref=src, dst_ref=dot_slots.at[d, s], send_sem=dot_send.at[d, s], recv_sem=dot_recv.at[d, s],
+            src_ref=src, dst_ref=dot_slots.at[d, s], send_sem=dot_send.at[d], recv_sem=dot_recv.at[s],
             device_id=to[d], device_id_type=MESH,
         )
+
+    def dotted(s, copies):
+        return bulk(dots.at[pl.ds(0, copies)], dot_send.at[0], dot_recv.at[s])
 
     def head_unit(u, carry):
         backward_unit(u)
@@ -318,25 +327,27 @@
     backward_unit(jnp.int32(GROUP))
 
     for i in range(CUTS // 2):
-        for r in range(4):
-            k = mine_of[r % 2][i]
-            scatter_local(r, 0, k).wait_recv()
-            add_local(r, 1, k)
-            scatter(r, 1, k).start()
-    dot_copy(0, 0, dot_slots.at[0, 0]).wait_recv()
+        for d in range(2):
+            k = mine_of[d][i]
+            scattered(d, 0, k).wait_recv()
+            for r in (d, d + 2):
+                add_local(r, 1, k)
+                scatter(r, 1, k).start()
+    dotted(0, 1).wait_recv()
     dot_slots[0, 0] = dot_slots[0, 0] + dots[dest(0, 1)]
     dot_copy(0, 1, dot_slots.at[0, 0]).start()
     backward_unit(jnp.int32(GROUP + 1))
 
     def rs_step(s, carry):
         for turn in range(CUTS):
-            for r in range(4):
-                k = (mine_of[1 - r % 2] + mine_of[r % 2])[turn]
-                scatter(r, s - 1, k).wait_recv()
-                add_local(r, s, k)
-                scatter(r, s, k).start()
+            for d in range(2):
+                k = (mine_of[1 - d] + mine_of[d])[turn]
+                scattered(d, s - 1, k).wait_recv()
+                for r in (d, d + 2):
+                    add_local(r, s, k)
+                    scatter(r, s, k).start()
+        dotted(s - 1, 2).wait_recv()
         for d in range(2):
-            dot_copy(d, s - 1, dot_slots.at[d, s - 1]).wait_recv()
             dot_slots[d, s - 1] = dot_slots[d, s - 1] + dots[dest(d, s)]
             dot_copy(d, s, dot_slots.at[d, s - 1]).start()
 
@@ -349,10 +360,10 @@
     lax.fori_loop(2, HOPS, rs_step, 0)
     last = HOPS - 1
     tiles = part // 128
-    for c in range(2):
-        for k in range(CUTS):
-            for d in range(2):
-                scatter(2 * c + d, last, k).wait_recv()
+    for k in range(CUTS):
+        for d in range(2):
+            scattered(d, last, k).wait_recv()
+        for c in range(2):
             lanes = slice(k * cut, (k + 1) * cut)
             total = running[2 * c, last, :, lanes].astype(F32) + running[2 * c + 1, last, :, lanes].astype(F32)
             total = total + local[c, spot[c], :, lanes].astype(F32)
@@ -362,66 +373,43 @@
     length = leave.shape[1]
     for i in range(2 * count):
         leave[i] = flat[i * length:(i + 1) * length, :].astype(BF)
-    for d in range(2):
-        dot_copy(d, last, dot_slots.at[d, last]).wait_recv()
+    dotted(last, 2).wait_recv()
     dot_out[...] = dot_slots[0, last] + dot_slots[1, last] + dots[spot[0]]
 
     def giveback(i, j, mine, src, dst):
         return pltpu.make_async_remote_copy(
             src_ref=src, dst_ref=dst,
-            send_sem=out_send.at[i, 2 * j + (0 if mine else 1)], recv_sem=out_recv.at[i, own_kind * count + e],
+            send_sem=out_send.at[i], recv_sem=out_recv.at[i],
             device_id=mate(j, mine), device_id_type=MESH,
         )
 
-    def returned(i, j, mine, ref):
-        kind, source = own_kind if mine else 1 - own_kind, rem(e + j, count)
-        return pltpu.make_async_remote_copy(
-            src_ref=ref.at[kind, source], dst_ref=ref.at[kind, source],
-            send_sem=out_send.at[i, 2 * j + (0 if mine else 1)], recv_sem=out_recv.at[i, kind * count + source],
-            device_id=mate(j, mine), device_id_type=MESH,
-        )
-
+    returned = [
+        bulk(ref.at[pl.ds(0, len(mates))], out_send.at[i], out_recv.at[i]) for i, ref in enumerate((leave, dots))
+    ]
     finals = [
         pltpu.make_async_copy(leave.at[my_slot], back_ref.at[own_kind, e], out_own.at[0]),
         pltpu.make_async_copy(dot_out, back_dots.at[own_kind, e], out_own.at[1]),
     ]
     for final in finals:
         final.start()
-    sent = []
     for j, mine in mates:
-        sent.append(giveback(0, j, mine, leave.at[column_slot(j, mine)], back_ref.at[own_kind, e]))
-        sent.append(giveback(1, j, mine, dot_out, back_dots.at[own_kind, e]))
-        sent[-2].start()
-        sent[-1].start()
+        giveback(0, j, mine, leave.at[column_slot(j, mine)], back_ref.at[own_kind, e]).start()
+        giveback(1, j, mine, dot_out, back_dots.at[own_kind, e]).start()
 
     for k in range(2):
-        for j, mine in mates:
-            bring(k, j, mine).wait_send()
+        brought(k).wait_send()
     for r in range(4):
-        gather(r, HOPS, r % 2, held(r, HOPS - 1)).wait_send()
-        for k in mine_of[r % 2]:
-            scatter_local(r, 0, k).wait_send()
-    dot_copy(0, 0, dots.at[dest(0, 0)]).wait_send()
-
-    def drain(s, carry):
-        for k in range(2):
-            for r in range(4):
-                gather(r, s, k, held(r, s - 1)).wait_send()
-        for k in range(CUTS):
-            for r in range(4):
-                scatter(r, s, k).wait_send()
-        for d in range(2):
-            dot_copy(d, s, dot_slots.at[d, s - 1]).wait_send()
-        return carry
-
-    lax.fori_loop(1, HOPS, drain, 0)
-    for copy in sent:
+        bulk(local.at[0, pl.ds(0, 2 * HOPS - 1)], ag_send.at[r], ag_recv.at[0, 0, 0]).wait_send()
+        bulk(local.at[0, 0, :, pl.ds(0, part // 2)], rs_first.at[r], rs_recv.at[0, 0, 0]).wait_send()
+        bulk(local.at[0, pl.ds(0, HOPS - 1)], rs_send.at[r], rs_recv.at[0, 0, 0]).wait_send()
+    for d in range(2):
+        bulk(dots.at[pl.ds(0, HOPS - d)], dot_send.at[d], dot_recv.at[0]).wait_send()
+    for copy in returned:
         copy.wait_send()
     for final in finals:
         final.wait()
-    for j, mine in mates:
-        returned(0, j, mine, back_ref).wait_recv()
-        returned(1, j, mine, back_dots).wait_recv()
+    for copy in returned:
+        copy.wait_recv()
 
 
 def run_experts(count, plan, tokens, out_grad, gate_weight, up_weight, down_weight):
@@ -459,17 +447,18 @@
             pltpu.VMEM((2, hidden, share), BF),
             pltpu.SemaphoreType.DMA((4,)),
             pltpu.SemaphoreType.DMA((2,)),
-            pltpu.SemaphoreType.DMA((2, 2 * count)),
-            pltpu.SemaphoreType.DMA((2, 2 * count)),
-            pltpu.SemaphoreType.DMA((4, HOPS + 1, 2)),
-            pltpu.SemaphoreType.DMA((4, HOPS + 1, 2)),
-            pltpu.SemaphoreType.DMA((4, HOPS, CUTS)),
-            pltpu.SemaphoreType.DMA((4, HOPS, CUTS)),
-            pltpu.SemaphoreType.DMA((2, HOPS)),
-            pltpu.SemaphoreType.DMA((2, HOPS)),
-            pltpu.SemaphoreType.DMA((2,)),
-            pltpu.SemaphoreType.DMA((2, 2 * count)),
-            pltpu.SemaphoreType.DMA((2, 2 * count)),
+            pltpu.SemaphoreType.DMA((2,)),
+            pltpu.SemaphoreType.DMA((2,)),
+            pltpu.SemaphoreType.DMA((4,)),
+            pltpu.SemaphoreType.DMA((2, HOPS + 1, 2)),
+            pltpu.SemaphoreType.DMA((4,)),
+            pltpu.SemaphoreType.DMA((4,)),
+            pltpu.SemaphoreType.DMA((2, HOPS, CUTS)),
+            pltpu.SemaphoreType.DMA((2,)),
+            pltpu.SemaphoreType.DMA((HOPS,)),
+            pltpu.SemaphoreType.DMA((2,)),
+            pltpu.SemaphoreType.DMA((2,)),
+            pltpu.SemaphoreType.DMA((2,)),
         ],
         compiler_params=pltpu.CompilerParams(
             collective_id=0, has_side_effects=True, vmem_limit_bytes=63 << 20

time: 211 us -> 204 us (0.967)
  Pallas kernels: 202 us -> 195 us
    pallas_call x1, Pallas kernels: 202 us -> 195 us  [run_experts(): pl.pallas_call(experts_kernel, out_shape=(jax.ShapeDtypeStruct((2, count,...]
where the time goes in v5:
time: 204 us; the launch traced here: 203 us
  Pallas kernels  195 us (96%)
  local copies, waits for them, and re-layouts  3.62 us (2%)
  other arithmetic  2.77 us (1%)
    pallas_call x1, Pallas kernels, run_experts(): pl.pallas_call(experts_kernel, out_shape=(jax.ShapeDtypeStruct((2, count,...  195 us

profile of v5, /device:TPU:1, one launch (start us, length us, event | category | flops | bytes accessed | tf_op | source)
XLA Modules:
  0.0 203.3 jit_solution(6604250649020116769)
XLA Ops:
  0.6 0.0 copy-start
  0.7 0.7 convert_bitcast_fusion
  1.4 0.8 slice_bitcast_fusion.1
  2.1 0.7 fusion.19
  2.8 0.1 copy.24
  2.9 0.6 select_maximum_fusion.plan_ref
  3.5 0.2 reduce_window_sum.11
  3.7 0.1 copy.25
  3.7 0.0 copy-start.1
  3.7 0.0 copy-start.2
  3.7 194.9 %experts.1 = (bf16[2,8,72,128]{3,2,1,0:T(8,128)(2,1)}, f32[2,8,8,128]{3,2,1,0:T(8,128)}) custom-call(f32[8,128]{1,0:T(8,128)} %select_maximum_fusion.plan_ref, bf16[8,6144]{1,0:T(8,128)(2,1)} %tok_ref.1, bf16[8,6144]{1,0:T(8,128)(2,1)} %grad_ref.1, bf16[1,6144,256]{2,1,0:T(8,128)(2,1)} %wg_hbm.1, bf16[1,6144,256]{2,1,0:T(8,128)(2,1)} %wu_hbm.1, ...), custom_call_target="tpu_custom_call" | custom-call | tf_op jit(solution)/shard_map/experts/pallas_call | solution.py:423
  198.6 0.8 slice.17
  199.4 0.1 constant_dynamic-slice_fusion
  199.5 0.1 copy.28
  199.6 0.1 copy.29
  199.6 0.0 copy-done
  199.6 0.0 copy-done.1
  199.6 0.2 select_reduce_fusion.4
  199.8 0.0 copy-done.2
  199.9 0.6 pad_maximum_fusion
  200.5 0.1 copy.26
  200.5 1.0 reshape.220
  201.6 0.4 copy.27
  202.0 0.2 dot_general.15
  202.2 0.2 convolution_bitcast_fusion
  202.4 0.9 fusion.1
  (7 shorter events, 0.1 us)
Async XLA Ops:
  0.6 199.0 %copy-start = (bf16[6144,8]{0,1:T(8,128)(2,1)S(1)}, bf16[6144,8]{0,1:T(8,128)(2,1)}, u32[]{:S(2)}) copy-start(bf16[6144,8]{0,1:T(8,128)(2,1)} %param.12) | copy-start | bytes 294916
  3.7 195.9 %copy-start.1 = (bf16[8,6144]{1,0:T(8,128)(2,1)S(1)}, bf16[8,6144]{1,0:T(8,128)(2,1)}, u32[]{:S(2)}) copy-start(bf16[8,6144]{1,0:T(8,128)(2,1)} %tok_ref.1) | copy-start | bytes 294916
  3.7 196.1 %copy-start.2 = (s32[8]{0:T(128)S(1)}, s32[8]{0:T(128)}, u32[]{:S(2)}) copy-start(s32[8]{0:T(128)} %param.10) | copy-start | bytes 100

commit v6 on v5

--- a/solution.py
+++ b/solution.py
@@ -47,13 +47,14 @@
 
 
 def experts_kernel(
-    plan_ref, tok_ref, grad_ref, wg_hbm, wu_hbm, wd_hbm, back_ref, back_dots,
-    send_ref, got, flat, leave, xs, running, local, acc_t, acc_g, grads, dots, dot_slots, dot_out, wg, wu, wd,
+    routes_ref, kept_ref, router_ref, tok_ref, grad_ref, wg_hbm, wu_hbm, wd_hbm, out_ref, gate_grad_ref,
+    back_ref, back_dots, send_ref, got, flat, leave, xs, running, local, acc_t, acc_g, grads, dots, dot_slots, dot_out, wg, wu, wd,
     w_sem, in_own, in_send, in_recv, ag_send, ag_recv, rs_first, rs_send, rs_recv, dot_send, dot_recv,
     out_own, out_send, out_recv,
 ):
     count = send_ref.shape[2]
-    capacity = 3 * tok_ref.shape[0] // 8
+    tokens = tok_ref.shape[0]
+    capacity = 3 * tokens // 8
     rows, share = xs.shape[2], xs.shape[3]
     hidden = wg.shape[1]
     part = share // 2
@@ -87,17 +88,22 @@
     for r in range(4):
         pl.semaphore_signal(barrier, inc=1, device_id=to[r], device_id_type=MESH)
     tiles = part // 128
-    row = lax.broadcasted_iota(jnp.int32, (count * capacity, 128), 0)
-    expert = jnp.zeros((count * capacity, 128), jnp.int32)
+    table = (count * capacity, tokens)
+    row = lax.broadcasted_iota(jnp.int32, table, 0)
+    expert = jnp.zeros(table, jnp.int32)
     for m in range(1, count):
         expert = expert + (row >= m * capacity).astype(jnp.int32)
-    place_in = (row - capacity * expert + 1).astype(F32)
-    expert = expert.astype(F32)
-    named = (plan_ref[0:1, :] == expert) | (plan_ref[1:2, :] == expert)
-    chosen = jnp.where(named, plan_ref[2:3, :], 0.0)
-    upto = lax.broadcasted_iota(jnp.int32, (128, 128), 0) <= lax.broadcasted_iota(jnp.int32, (128, 128), 1)
-    nth = jnp.dot(chosen.astype(BF), upto.astype(F32).astype(BF), preferred_element_type=F32)
-    pick = jnp.where(nth == place_in, chosen, 0.0).astype(BF)[:, : tok_ref.shape[0]]
+    slot_of = row - capacity * expert
+    kept = kept_ref[...].astype(F32)
+    is_first = routes_ref[0:1, :] == expert
+    is_second = routes_ref[1:2, :] == expert
+    chosen = jnp.where(is_first | is_second, 1.0, 0.0) * kept
+    square = (tokens, tokens)
+    down, across = lax.broadcasted_iota(jnp.int32, square, 0), lax.broadcasted_iota(jnp.int32, square, 1)
+    upto = jnp.where(down <= across, 1.0, 0.0).astype(BF)
+    nth = jnp.dot(chosen.astype(BF), upto, preferred_element_type=F32)
+    pick_full = jnp.where(nth == (slot_of + 1).astype(F32), chosen, 0.0)
+    pick = pick_full.astype(BF)
     length = send_ref.shape[3]
     for kind, source in enumerate((tok_ref, grad_ref)):
         for c in range(2):
@@ -111,6 +117,19 @@
             for i in range(count):
                 begin = (k * count + i) * length
                 send_ref[kind, k, i] = flat[begin:begin + length, :].astype(BF)
+
+    logits = dot_nt(router_ref[...], tok_ref[...])
+    ids = lax.broadcasted_iota(jnp.int32, (count, tokens), 0)
+    first_hot = jnp.where(routes_ref[0:1, :] == ids, 1.0, 0.0)
+    second_hot = jnp.where(routes_ref[1:2, :] == ids, 1.0, 0.0)
+    first_logit = jnp.sum(logits * first_hot, axis=0, keepdims=True)
+    second_logit = jnp.sum(logits * second_hot, axis=0, keepdims=True)
+    gate_first = jax.nn.sigmoid(first_logit - second_logit)
+    gate_second = jax.nn.sigmoid(second_logit - first_logit)
+    eye = jnp.where(down == across, 1.0, 0.0).astype(BF)
+    gate_of = jnp.where(is_first, gate_first, gate_second)
+    weigh = dot_nt(eye, (pick_full * gate_of).astype(BF)).astype(BF)
+    keep_column = dot_nt(eye, jnp.broadcast_to(kept, (128, tokens)).astype(BF))[:, 0:1]
 
     pl.semaphore_wait(barrier, len(mates) + 4)
 
@@ -411,8 +430,37 @@
     for copy in returned:
         copy.wait_recv()
 
-
-def run_experts(count, plan, tokens, out_grad, gate_weight, up_weight, down_weight):
+    for i in range(count):
+        flat[i * capacity:(i + 1) * capacity, :] = back_dots[0, i, 0:capacity, :]
+    lane = lax.broadcasted_iota(jnp.int32, (count * capacity, 128), 1)
+    row = lax.broadcasted_iota(jnp.int32, (count * capacity, 128), 0)
+    wanted = row + capacity * my_slot
+    for m in range(1, count):
+        wanted = wanted - capacity * (row >= m * capacity).astype(jnp.int32)
+    dot_column = jnp.where(lane == wanted, flat[0:count * capacity, :], 0.0)
+    dot_column = jnp.sum(dot_column, axis=1, keepdims=True)
+    dot_first = jnp.sum(jnp.where(is_first, pick_full, 0.0) * dot_column, axis=0, keepdims=True)
+    dot_second = jnp.sum(jnp.where(is_second, pick_full, 0.0) * dot_column, axis=0, keepdims=True)
+    product = gate_first * gate_second * kept
+    grad_first = product * (dot_first - dot_second)
+    grad_second = product * (dot_second - dot_first)
+    gate_grad_ref[0:1, :] = grad_first
+    gate_grad_ref[1:2, :] = grad_second
+    logit_grad = first_hot * grad_first + second_hot * grad_second
+    high = logit_grad.astype(BF)
+    low = (logit_grad - high.astype(F32)).astype(BF)
+    pieces = jnp.concatenate([dot_nt(eye, high), dot_nt(eye, low)], axis=0).astype(BF)
+    for kind in range(2):
+        for i in range(count):
+            flat[i * length:(i + 1) * length, :] = back_ref[kind, i].astype(F32)
+        parts = [flat[pl.ds(i, count * capacity, stride=2 * tiles), :].astype(BF) for i in range(2 * tiles)]
+        total = jnp.dot(weigh, jnp.concatenate(parts, axis=1), preferred_element_type=F32)
+        lanes = slice(kind * half, (kind + 1) * half)
+        term = jnp.dot(pieces, router_ref[:, lanes], preferred_element_type=F32)
+        out_ref[:, lanes] = ((total + (term[:tokens] + term[tokens:])) * keep_column).astype(BF)
+
+
+def run_experts(count, routes, kept, router, tokens, out_grad, gate_weight, up_weight, down_weight):
     width, hidden = gate_weight.shape[1:]
     share, part = width // 2, width // 4
     capacity = 3 * tokens.shape[0] // 8
@@ -423,12 +471,14 @@
     return pl.pallas_call(
         experts_kernel,
         out_shape=(
-            jax.ShapeDtypeStruct((2, count, length, 128), BF),
-            jax.ShapeDtypeStruct((2, count, 8, 128), F32),
+            jax.ShapeDtypeStruct(tokens.shape, BF),
+            jax.ShapeDtypeStruct(routes.shape, F32),
         ),
-        in_specs=[vmem, vmem, vmem, hbm, hbm, hbm],
+        in_specs=[vmem, vmem, vmem, vmem, vmem, hbm, hbm, hbm],
         out_specs=(vmem, vmem),
         scratch_shapes=[
+            pltpu.VMEM((2, count, length, 128), BF),
+            pltpu.VMEM((2, count, 8, 128), F32),
             pltpu.VMEM((2, 2, count, length, 128), BF),
             pltpu.VMEM((2, 2 * count, length, 128), BF),
             pltpu.VMEM((2 * count * length, 128), F32),
@@ -464,50 +514,15 @@
             collective_id=0, has_side_effects=True, vmem_limit_bytes=63 << 20
         ),
         name="experts",
-    )(plan, tokens, out_grad, gate_weight, up_weight, down_weight)
+    )(routes, kept, router, tokens, out_grad, gate_weight, up_weight, down_weight)
 
 
 def on_device(tokens, out_grad, kept_mask, routes, router, gate_weight, up_weight, down_weight):
-    row_count, width = tokens.shape
-    count = lax.axis_size("expert")
-    capacity = 3 * row_count // 8
-    columns = lax.broadcasted_iota(jnp.int32, (row_count, count), 1)
-    first_hot = (routes[:, 0:1] == columns).astype(F32)
-    second_hot = (routes[:, 1:2] == columns).astype(F32)
-    keep_rows = kept_mask.astype(F32)
-    chosen = ((first_hot + second_hot) * keep_rows[:, None]).astype(jnp.int32)
-    position = jnp.cumsum(chosen, axis=0) - 1
-    slot_iota = lax.broadcasted_iota(jnp.int32, (row_count, count, capacity), 2)
-    select_mask = (chosen[:, :, None] == 1) & (position[:, :, None] == slot_iota)
-    select_bf = select_mask.astype(BF)
-    select_full = select_mask.astype(F32)
-    plan = jnp.concatenate([routes.astype(F32).T, keep_rows[None]], axis=0)
-    plan = jnp.pad(plan, ((0, 5), (0, 128 - row_count)))
-    back, back_dots = run_experts(count, plan, tokens, out_grad, gate_weight, up_weight, down_weight)
-    back = back.reshape(2, count, capacity, width // 2)
-    own_slot = rem(lax.axis_index("mp"), 2) * count + lax.axis_index("expert")
-    dot_back = lax.dynamic_slice_in_dim(back_dots[0, :, 0, :], own_slot * capacity, capacity, 1)
-
-    logits = jnp.dot(tokens, router, preferred_element_type=F32)
-    first_logit = jnp.sum(logits * first_hot, axis=1)
-    second_logit = jnp.sum(logits * second_hot, axis=1)
-    gate_first = jax.nn.sigmoid(first_logit - second_logit)
-    gate_second = jax.nn.sigmoid(second_logit - first_logit)
-    gate_table = (first_hot * gate_first[:, None] + second_hot * gate_second[:, None]).astype(BF)
-    weigh = select_bf * gate_table[:, :, None]
-    expert_sum = jnp.einsum("tec,kecd->tkd", weigh, back, preferred_element_type=F32)
-    expert_sum = expert_sum.reshape(row_count, width)
-    dot_table = jnp.sum(select_full * dot_back[None], axis=2)
-    dot_first = jnp.sum(dot_table * first_hot, axis=1)
-    dot_second = jnp.sum(dot_table * second_hot, axis=1)
-    product = gate_first * gate_second * keep_rows
-    grad_first = product * (dot_first - dot_second)
-    grad_second = product * (dot_second - dot_first)
-    logit_grad = first_hot * grad_first[:, None] + second_hot * grad_second[:, None]
-    router_term = jnp.dot(logit_grad, router.astype(F32).T, precision=lax.Precision.HIGHEST)
-    d_tokens = ((expert_sum + router_term) * keep_rows[:, None]).astype(BF)
-    gate_grad = jnp.stack([grad_first, grad_second], axis=1)
-    return (d_tokens, gate_grad)
+    d_tokens, gate_grad = run_experts(
+        lax.axis_size("expert"), routes.T, kept_mask[None], router.T, tokens, out_grad,
+        gate_weight, up_weight, down_weight,
+    )
+    return (d_tokens, gate_grad.T)
 
 
 def solution(mesh):

time: 204 us -> 199 us (0.975)
  other arithmetic: 2.77 us -> 0 us
    unnamed x6 -> x2, local copies, waits for them, and re-layouts: 0.02 us -> 2.78 us
where the time goes in v6:
time: 199 us
  Pallas kernels  195 us (98%)
  local copies, waits for them, and re-layouts  2.78 us (1%)
    pallas_call x1, Pallas kernels, run_experts(): pl.pallas_call(experts_kernel, out_shape=(jax.ShapeDtypeStruct(tokens.sha...  195 us

profile of v6, /device:TPU:1, one launch (start us, length us, event | category | flops | bytes accessed | tf_op | source)
XLA Modules:
  0.0 198.8 jit_solution(3036225209298427280)
XLA Ops:
  0.6 195.4 %experts.1 = (bf16[8,6144]{1,0:T(8,128)(2,1)}, f32[2,8]{1,0:T(2,128)}) custom-call(s32[2,8]{1,0:T(2,128)} %bitcast.5, s32[1,8]{1,0:T(1,128)} %bitcast.7, bf16[8,6144]{1,0:T(8,128)(2,1)} %bitcast.4, bf16[8,6144]{1,0:T(8,128)(2,1)} %tok_ref.1, bf16[8,6144]{1,0:T(8,128)(2,1)} %grad_ref.1, bf16[1,6144,256]{2,1,0:T(8,128)(2,1)} %wg_hbm.1, ...), custom_call_target="tpu_custom_call" | custom-call | tf_op jit(solution)/shard_map/experts/pallas_call | solution.py:471
  196.1 1.5 copy.12
  197.6 1.2 copy.13

commit v7 on v6

--- a/solution.py
+++ b/solution.py
@@ -48,7 +48,7 @@
 
 def experts_kernel(
     routes_ref, kept_ref, router_ref, tok_ref, grad_ref, wg_hbm, wu_hbm, wd_hbm, out_ref, gate_grad_ref,
-    back_ref, back_dots, send_ref, got, flat, leave, xs, running, local, acc_t, acc_g, grads, dots, dot_slots, dot_out, wg, wu, wd,
+    back_ref, back_dots, send_ref, got, flat, leave, xs, running, first, local, acc_t, acc_g, grads, dots, dot_slots, dot_out, wg, wu, wd,
     w_sem, in_own, in_send, in_recv, ag_send, ag_recv, rs_first, rs_send, rs_recv, dot_send, dot_recv,
     out_own, out_send, out_recv,
 ):
@@ -188,19 +188,12 @@
     for load in loads:
         load.wait()
 
-    def forward_unit(unit):
-        b = div(unit, 4)
-        c = div(rem(unit, 4), 2)
-        kind = rem(unit, 2)
-        p = spot[0] * (1 - c) + spot[1] * c
+    def forward(c, kind, low, high, each):
         begin = pl.multiple_of(c * share, share)
 
         def positions(parity):
-            low = p - GROUP * (b + 1)
-            low = low + rem(low + parity + 2 * RING, 2) + RING
-            high = p + GROUP * b
-            high = high + rem(high + parity, 2)
-            return [div(rem(q, RING), 2) for q in (low, low + 2, high, high + 2)]
+            runs = [run + rem(run + parity, 2) for run in (low + 2 * RING, high + 2 * RING)]
+            return [div(rem(run + 2 * i, RING), 2) for run in runs for i in range(each)]
 
         @pl.when(kind == 0)
         def _():
@@ -219,6 +212,25 @@
             grad = dot_nt(lhs, wd[c])
             for i, t in enumerate(where):
                 acc_g[c, t] = grad[i * rows:(i + 1) * rows]
+
+    def forward_unit(unit):
+        b = div(unit, 4)
+        c = div(rem(unit, 4), 2)
+        p = spot[0] * (1 - c) + spot[1] * c
+        forward(c, rem(unit, 2), p - GROUP * (b + 1), p + GROUP * b, 2)
+
+    def forward_half(unit):
+        h = div(unit, 4)
+        c = div(rem(unit, 4), 2)
+        p = spot[0] * (1 - c) + spot[1] * c
+        forward(c, rem(unit, 2), p - (HOPS - 2) - 2 * h, p + HOPS - GROUP + 2 * h, 1)
+
+    def half_units(begin, end):
+        def body(u, carry):
+            forward_half(u)
+            return carry
+
+        lax.fori_loop(begin, end, body, 0)
 
     def gathered(d, s, k):
         return bulk(local.at[0, pl.ds(0, 2)], ag_send.at[d], ag_recv.at[d, s, k])
@@ -239,17 +251,17 @@
         def _():
             forward_unit(s - GROUP)
 
+        @pl.when(s >= HOPS - 2)
+        def _():
+            half_units(2 * (s - (HOPS - 2)), 2 * (s - (HOPS - 2)) + 2)
+
         return carry
 
     lax.fori_loop(1, HOPS, ag_step, 0)
     for d in range(2):
         gathered(d, HOPS, d).wait_recv()
 
-    def tail_unit(u, carry):
-        forward_unit(u)
-        return carry
-
-    lax.fori_loop(HOPS - GROUP, HOPS, tail_unit, 0)
+    half_units(4, 8)
 
     ones = jnp.ones((8, 128), F32)
     for pair in range(16):
@@ -301,16 +313,18 @@
     cut = part // CUTS
     mine_of = [[d * (CUTS // 2) + i for i in range(CUTS // 2)] for d in range(2)]
 
-    def scatter(r, s, k, src=None, first=False):
+    def scatter(r, s, k, src=None, opening=False):
         lanes = pl.ds(k * cut, cut)
         return pltpu.make_async_remote_copy(
             src_ref=running.at[r, s - 1, :, lanes] if src is None else src, dst_ref=running.at[r, s, :, lanes],
-            send_sem=(rs_first if first else rs_send).at[r], recv_sem=rs_recv.at[r % 2, s, k],
+            send_sem=(rs_first if opening else rs_send).at[r], recv_sem=rs_recv.at[r % 2, s, k],
             device_id=to[r], device_id_type=MESH,
         )
 
     def scatter_local(r, s, k):
-        return scatter(r, s, k, local.at[r // 2, dest(r, s), :, pl.ds(k * cut, cut)], s == 0)
+        lanes = pl.ds(k * cut, cut)
+        src = first.at[r // 2, :, lanes] if s == 0 else local.at[r // 2, dest(r, s), :, lanes]
+        return scatter(r, s, k, src, s == 0)
 
     def scattered(d, s, k):
         return bulk(running.at[pl.ds(0, 2), 0, :, pl.ds(0, cut)], rs_send.at[d], rs_recv.at[d, s, k])
@@ -334,10 +348,16 @@
         return carry
 
     for c in range(2):
-        lax.fori_loop(2 * c, 2 * c + 2, head_unit, 0)
+        q = dest(2 * c, 0)
+        begin = pl.multiple_of(rem(q, 2) * half + c * part, part)
+        y = dot_nt(grads[c, q, :, :hidden], wg[pl.ds(begin, part), :])
+        y = y + dot_nt(grads[c, q, :, hidden:], wu[pl.ds(begin, part), :])
+        first[c] = y.astype(BF)
         for r in (2 * c, 2 * c + 1):
             for k in mine_of[r % 2]:
                 scatter_local(r, 0, k).start()
+    for c in range(2):
+        lax.fori_loop(2 * c, 2 * c + 2, head_unit, 0)
         for r in (2 * c, 2 * c + 1):
             for k in mine_of[1 - r % 2]:
                 scatter_local(r, 1, k).start()
@@ -377,6 +397,21 @@
         return carry
 
     lax.fori_loop(2, HOPS, rs_step, 0)
+    def giveback(i, j, mine, src, dst):
+        return pltpu.make_async_remote_copy(
+            src_ref=src, dst_ref=dst,
+            send_sem=out_send.at[i], recv_sem=out_recv.at[i],
+            device_id=mate(j, mine), device_id_type=MESH,
+        )
+
+    returned = [
+        bulk(ref.at[pl.ds(0, len(mates))], out_send.at[i], out_recv.at[i]) for i, ref in enumerate((leave, dots))
+    ]
+    finals = [
+        pltpu.make_async_copy(leave.at[my_slot], back_ref.at[own_kind, e], out_own.at[0]),
+        pltpu.make_async_copy(dot_out, back_dots.at[own_kind, e], out_own.at[1]),
+    ]
+
     last = HOPS - 1
     tiles = part // 128
     for k in range(CUTS):
@@ -389,31 +424,17 @@
             for j in range(tiles // CUTS):
                 line = c * tiles + k * (tiles // CUTS) + j
                 flat[pl.ds(line, rows, stride=2 * tiles), :] = total[:, j * 128:(j + 1) * 128]
+    dotted(last, 2).wait_recv()
+    dot_out[...] = dot_slots[0, last] + dot_slots[1, last] + dots[spot[0]]
+    finals[1].start()
+    for j, mine in mates:
+        giveback(1, j, mine, dot_out, back_dots.at[own_kind, e]).start()
     length = leave.shape[1]
     for i in range(2 * count):
         leave[i] = flat[i * length:(i + 1) * length, :].astype(BF)
-    dotted(last, 2).wait_recv()
-    dot_out[...] = dot_slots[0, last] + dot_slots[1, last] + dots[spot[0]]
-
-    def giveback(i, j, mine, src, dst):
-        return pltpu.make_async_remote_copy(
-            src_ref=src, dst_ref=dst,
-            send_sem=out_send.at[i], recv_sem=out_recv.at[i],
-            device_id=mate(j, mine), device_id_type=MESH,
-        )
-
-    returned = [
-        bulk(ref.at[pl.ds(0, len(mates))], out_send.at[i], out_recv.at[i]) for i, ref in enumerate((leave, dots))
-    ]
-    finals = [
-        pltpu.make_async_copy(leave.at[my_slot], back_ref.at[own_kind, e], out_own.at[0]),
-        pltpu.make_async_copy(dot_out, back_dots.at[own_kind, e], out_own.at[1]),
-    ]
-    for final in finals:
-        final.start()
+    finals[0].start()
     for j, mine in mates:
         giveback(0, j, mine, leave.at[column_slot(j, mine)], back_ref.at[own_kind, e]).start()
-        giveback(1, j, mine, dot_out, back_dots.at[own_kind, e]).start()
 
     for k in range(2):
         brought(k).wait_send()
@@ -423,13 +444,9 @@
         bulk(local.at[0, pl.ds(0, HOPS - 1)], rs_send.at[r], rs_recv.at[0, 0, 0]).wait_send()
     for d in range(2):
         bulk(dots.at[pl.ds(0, HOPS - d)], dot_send.at[d], dot_recv.at[0]).wait_send()
-    for copy in returned:
-        copy.wait_send()
-    for final in finals:
-        final.wait()
-    for copy in returned:
-        copy.wait_recv()
-
+    returned[1].wait_send()
+    finals[1].wait()
+    returned[1].wait_recv()
     for i in range(count):
         flat[i * capacity:(i + 1) * capacity, :] = back_dots[0, i, 0:capacity, :]
     lane = lax.broadcasted_iota(jnp.int32, (count * capacity, 128), 1)
@@ -450,6 +467,9 @@
     high = logit_grad.astype(BF)
     low = (logit_grad - high.astype(F32)).astype(BF)
     pieces = jnp.concatenate([dot_nt(eye, high), dot_nt(eye, low)], axis=0).astype(BF)
+    returned[0].wait_send()
+    finals[0].wait()
+    returned[0].wait_recv()
     for kind in range(2):
         for i in range(count):
             flat[i * length:(i + 1) * length, :] = back_ref[kind, i].astype(F32)
@@ -485,6 +505,7 @@
             pltpu.VMEM((2 * count, length, 128), BF),
             pltpu.VMEM((2, RING, rows, share), BF),
             pltpu.VMEM((4, HOPS, rows, part), BF),
+            pltpu.VMEM((2, rows, part), BF),
             pltpu.VMEM((2, RING, rows, part), BF),
             pltpu.VMEM((2, 16, rows, 2 * hidden), F32),
             pltpu.VMEM((2, 16, rows, hidden), F32),

time: 199 us -> 197 us (0.990)
  Pallas kernels: 195 us -> 193 us
    pallas_call x1, Pallas kernels: 195 us -> 193 us  [run_experts(): pl.pallas_call(experts_kernel, out_shape=(jax.ShapeDtypeStruct(tokens.sha...]
where the time goes in v7:
time: 197 us
  Pallas kernels  193 us (98%)
  local copies, waits for them, and re-layouts  2.78 us (1%)
    pallas_call x1, Pallas kernels, run_experts(): pl.pallas_call(experts_kernel, out_shape=(jax.ShapeDtypeStruct(tokens.sha...  193 us

profile of v7, /device:TPU:1, one launch (start us, length us, event | category | flops | bytes accessed | tf_op | source)
XLA Modules:
  0.0 196.8 jit_solution(11625273909362457027)
XLA Ops:
  0.6 193.4 %experts.1 = (bf16[8,6144]{1,0:T(8,128)(2,1)}, f32[2,8]{1,0:T(2,128)}) custom-call(s32[2,8]{1,0:T(2,128)} %bitcast.5, s32[1,8]{1,0:T(1,128)} %bitcast.7, bf16[8,6144]{1,0:T(8,128)(2,1)} %bitcast.4, bf16[8,6144]{1,0:T(8,128)(2,1)} %tok_ref.1, bf16[8,6144]{1,0:T(8,128)(2,1)} %grad_ref.1, bf16[1,6144,256]{2,1,0:T(8,128)(2,1)} %wg_hbm.1, ...), custom_call_target="tpu_custom_call" | custom-call | tf_op jit(solution)/shard_map/experts/pallas_call | solution.py:491
  194.0 1.5 copy.12
  195.6 1.2 copy.13

commit v8 on v7

--- a/solution.py
+++ b/solution.py
@@ -13,7 +13,7 @@
 RING = 32
 HOPS = 16
 GROUP = 4
-CUTS = 4
+CUTS = 6
 
 
 def div(a, b):

time: 197 us -> 196 us (level)
  no operation moved by 1% of the time
where the time goes in v8:
time: 196 us
  Pallas kernels  192 us (98%)
  local copies, waits for them, and re-layouts  2.78 us (1%)
    pallas_call x1, Pallas kernels, run_experts(): pl.pallas_call(experts_kernel, out_shape=(jax.ShapeDtypeStruct(tokens.sha...  192 us

profile of v8, /device:TPU:1, one launch (start us, length us, event | category | flops | bytes accessed | tf_op | source)
XLA Modules:
  0.0 195.7 jit_solution(7627826443310734433)
XLA Ops:
  0.6 192.3 %experts.1 = (bf16[8,6144]{1,0:T(8,128)(2,1)}, f32[2,8]{1,0:T(2,128)}) custom-call(s32[2,8]{1,0:T(2,128)} %bitcast.5, s32[1,8]{1,0:T(1,128)} %bitcast.7, bf16[8,6144]{1,0:T(8,128)(2,1)} %bitcast.4, bf16[8,6144]{1,0:T(8,128)(2,1)} %tok_ref.1, bf16[8,6144]{1,0:T(8,128)(2,1)} %grad_ref.1, bf16[1,6144,256]{2,1,0:T(8,128)(2,1)} %wg_hbm.1, ...), custom_call_target="tpu_custom_call" | custom-call | tf_op jit(solution)/shard_map/experts/pallas_call | solution.py:491
  193.0 1.5 copy.12
  194.5 1.2 copy.13
